TPU v7x, 256 devices: a whole 4x4x8 slice. The times are simulated.
256 devices in a mesh: tm: 128 (over z, x, y_hi, core), sec: 2 (over y_lo).
Axes of the slice: x: 4, y: 4 (y_hi: 2, y_lo: 2; y = y_hi * 2 + y_lo), z: 8, core: 2. Of those that a mesh axis runs over, the one named last changes fastest.
Arguments:
- state: float32 [512, 6, 4, 32, 128], P('tm', None, None, 'sec'), may hold values from 0.05 to 1
- adjoint: float32 [512, 6, 4, 32, 128], P('tm', None, None, 'sec'), may hold values from -6 to 6
- plan: int32 [512, 4], P('tm'), may hold values from 1 to 3
- valve: int32 [512, 4], P('tm'), may hold values 0 or 1
Outputs:
- residual: float32 [512, 6, 4, 32, 128], P('tm', None, None, 'sec')
- adjoint_out: float32 [512, 6, 4, 32, 128], P('tm', None, None, 'sec')
Inputs may be any that keep to these rules, and one draw needn't show every extreme that they name: Bed b at instance t takes purge gas from bed (b + plan) mod 4, never from itself.
All inputs are finite; a program needn't handle non-finite values. No bound on the sum of `valve` on one device may be relied on, other than what follows from the above.
Results may differ from a plain program's by a relative error of at most 0.0003.
Values sent between devices are 32-bit elements; how exact they have to be, the bound alone decides.
A program may use at most 64 MiB of HBM per device.

v0:
```python
import jax
import jax.numpy as jnp
from jax import lax
from jax.sharding import PartitionSpec as P

STENCIL = (0.8, -0.2, 4.0 / 105.0, -1.0 / 280.0)
TIME_SCALE = 4.0
FLOW_VELOCITY = 1.0
AXIAL_DISPERSION = 0.3
RADIAL_SPREADING = 0.2
BINDING_STRENGTH = (1.5, 0.6)
HEAT_EXPONENT = (0.5, 0.3)
KINETIC = (1.2, 0.7)
CAPACITY = (2.0, 1.0)
SORPTION_HEAT = (0.4, 0.25)
PURGE_GAIN = 1.5


def extended_2(cells, sides, width, closed):
    for axis, dim in sides:
        count = lax.axis_size(axis)
        ends = count if closed else count - 1
        head = lax.slice_in_dim(cells, 0, width, axis=dim)
        tail = lax.slice_in_dim(cells, cells.shape[dim] - width, cells.shape[dim], axis=dim)
        cells = jnp.concatenate(
            [
                lax.ppermute(tail, axis, [(i, (i + 1) % count) for i in range(ends)]),
                cells,
                lax.ppermute(head, axis, [((i + 1) % count, i) for i in range(ends)]),
            ],
            axis=dim,
        )
    return cells


def radial_diffusion_term(field):
    zero_edge = jnp.zeros_like(field[..., :1])
    upper = jnp.concatenate([field[..., 1:], zero_edge], axis=-1)
    lower = jnp.concatenate([zero_edge, field[..., :-1]], axis=-1)
    return upper - 2.0 * field + lower


def time_derivative(extended, instances):
    total_sum = jnp.zeros_like(extended[4 : 4 + instances])
    for offset, weight in enumerate(STENCIL):
        shift_by = offset + 1
        total_sum = total_sum + weight * (
            extended[4 + shift_by : 4 + shift_by + instances]
            - extended[4 - shift_by : 4 - shift_by + instances]
        )
    return TIME_SCALE * total_sum


def spatial_residual(padded, offsets, valves, purge_mask):
    middle_cell = padded[:, :, :, 1:-1]
    cell_underneath = padded[:, :, :, :-2]
    cell_overhead = padded[:, :, :, 2:]
    gas_part = middle_cell[:, 0:3]
    transport = FLOW_VELOCITY * (gas_part - cell_underneath[:, 0:3]) - AXIAL_DISPERSION * (
        cell_overhead[:, 0:3] - 2.0 * gas_part + cell_underneath[:, 0:3]
    )
    gas_res = transport - RADIAL_SPREADING * radial_diffusion_term(gas_part)
    thermal_field = middle_cell[:, 5]
    binding_first = BINDING_STRENGTH[0] * jnp.exp(HEAT_EXPONENT[0] * thermal_field)
    binding_second = BINDING_STRENGTH[1] * jnp.exp(HEAT_EXPONENT[1] * thermal_field)
    denominator = 1.0 + binding_first * middle_cell[:, 0] + binding_second * middle_cell[:, 1]
    uptake_first = KINETIC[0] * (
        CAPACITY[0] * binding_first * middle_cell[:, 0] / denominator - middle_cell[:, 3]
    )
    uptake_second = KINETIC[1] * (
        CAPACITY[1] * binding_second * middle_cell[:, 1] / denominator - middle_cell[:, 4]
    )
    bed_count = padded.shape[2]
    bed_ids = jnp.arange(bed_count, dtype=jnp.int32)
    product = jnp.sum(gas_part * purge_mask[None, None, None, :, None], axis=3)
    source = (bed_ids[None, :] + offsets) % bed_count
    lookup_table = (source[:, :, None] == bed_ids[None, None, :]).astype(jnp.float32)
    incoming = jnp.sum(lookup_table[:, None, :, :, None] * product[:, :, None, :, :], axis=3)
    purge_term = PURGE_GAIN * valves.astype(jnp.float32)[:, None, :, None] * (product - incoming)
    gas_res = gas_res + purge_term[:, :, :, None, :] * purge_mask[None, None, None, :, None]
    energy_residual = FLOW_VELOCITY * (thermal_field - cell_underneath[:, 5]) - AXIAL_DISPERSION * (
        cell_overhead[:, 5] - 2.0 * thermal_field + cell_underneath[:, 5]
    )
    energy_residual = (
        energy_residual
        - RADIAL_SPREADING * radial_diffusion_term(thermal_field)
        - (SORPTION_HEAT[0] * uptake_first + SORPTION_HEAT[1] * uptake_second)
    )
    rows = [
        gas_res[:, 0] + uptake_first,
        gas_res[:, 1] + uptake_second,
        gas_res[:, 2],
        -uptake_first,
        -uptake_second,
        energy_residual,
    ]
    return jnp.stack(rows, axis=1)


def local(state, adjoint, plan, valve):
    instances = state.shape[0]
    cells_axial = state.shape[3]
    on_last = lax.axis_index("sec") == lax.axis_size("sec") - 1
    state_ext = extended_2(state, (("tm", 0),), 4, True)
    adjoint_ext = extended_2(adjoint, (("tm", 0),), 4, True)
    state_time = time_derivative(state_ext, instances)
    adjoint_time = time_derivative(adjoint_ext, instances)
    padded = extended_2(state, (("sec", 3),), 1, False)
    purge_mask = jnp.logical_and(
        jnp.arange(cells_axial, dtype=jnp.int32) == cells_axial - 1, on_last
    ).astype(jnp.float32)
    forward, pullback = jax.vjp(
        lambda field: spatial_residual(field, plan, valve, purge_mask), padded
    )
    pulled = pullback(adjoint)[0]
    edge_cells = jnp.concatenate([pulled[:, :, :, :1], pulled[:, :, :, -1:]], axis=3)
    arrived = extended_2(edge_cells, (("sec", 3),), 1, False)
    local_adj = pulled[:, :, :, 1:-1]
    local_adj = local_adj.at[:, :, :, 0].add(arrived[:, :, :, 0])
    local_adj = local_adj.at[:, :, :, -1].add(arrived[:, :, :, 3])
    return (state_time + forward, local_adj - adjoint_time)


def solution(mesh):
    return jax.shard_map(
        local,
        mesh=mesh,
        in_specs=(
            P("tm", None, None, "sec", None),
            P("tm", None, None, "sec", None),
            P("tm", None),
            P("tm", None),
        ),
        out_specs=(P("tm", None, None, "sec", None), P("tm", None, None, "sec", None)),
        check_vma=False,
    )
```

profile of v0, /device:TPU:18, one launch (start us, length us, event | category | flops | bytes accessed | tf_op | source)
XLA Modules:
  0.0 74.4 jit_solution(14812259480644251599)
XLA Ops:
  0.7 3.2 %collective-permute-start.6 = (f32[4,6,4,16,128]{4,3,2,1,0:T(8,128)}, f32[4,6,4,16,128]{4,3,2,1,0:T(8,128)}, u32[]{:S(2)}, u32[]{:S(2)}) collective-permute-start(f32[4,6,4,16,128]{4,3,2,1,0:T(8,128)} %param.9), channel_id=1, source_target_pairs={{2,0},{4,2},{6,4},{8,6},{10,8},{12,10},{14,12},{16,14},{18,16},{20... | collective-permute-start | bytes 2359304 | tf_op jit(solution)/shard_map/ppermute | solution.py:29
  4.0 2.3 %fusion.71 = (f32[4,6,4,16,128]{4,3,2,0,1:T(8,128)S(1)}, f32[4,6,4,17,128]{4,3,2,0,1:T(8,128)}) fusion(f32[4,6,4,16,128]{4,3,2,1,0:T(8,128)} %param.8), kind=kLoop, calls=%fused_computation.155 | loop fusion | bytes 2359296 | tf_op args[0]
  6.9 1.3 %collective-permute-start.3 = (f32[4,6,4,1,128]{4,3,2,0,1:T(1,128)}, f32[4,6,4,1,128]{4,3,2,0,1:T(1,128)}, u32[]{:S(2)}, u32[]{:S(2)}) collective-permute-start(f32[4,6,4,1,128]{4,3,2,0,1:T(1,128)} %get-tuple-element.62), channel_id=1, source_target_pairs={{1,0},{3,2},{5,4},{7,6},{9,8},{11,10},{13,12},{15,14},{17,16},{19,... | collective-permute-start | bytes 147464 | tf_op jit(solution)/shard_map/ppermute | solution.py:29
  8.2 5.8 %collective-permute-start.2 = (f32[4,6,4,1,128]{4,3,2,0,1:T(1,128)}, f32[4,6,4,1,128]{4,3,2,0,1:T(1,128)}, u32[]{:S(2)}, u32[]{:S(2)}) collective-permute-start(f32[4,6,4,1,128]{4,3,2,0,1:T(1,128)} %get-tuple-element.61), channel_id=1, source_target_pairs={{0,1},{2,3},{4,5},{6,7},{8,9},{10,11},{12,13},{14,15},{16,17},{18,... | collective-permute-start | bytes 147464 | tf_op jit(solution)/shard_map/ppermute | solution.py:27
  14.0 0.9 %bitcast_negate_fusion.3 = (f32[4,1,4,16,128]{4,3,2,0,1:T(8,128)}, f32[4,1,4,16,128]{4,3,2,0,1:T(8,128)}, f32[4,1,4,16,128]{4,3,2,0,1:T(8,128)}, f32[4,1,4,16,12...) fusion(f32[4,6,4,16,128]{4,3,2,1,0:T(8,128)S(1)} %copy-done), kind=kLoop, calls=%fused_computation.70 | loop fusion | flops 458752 | bytes 1441792 | tf_op jit(solution)/shard_map/transpose(jvp())/neg | solution.py:81
  15.5 1.4 %fusion.70 = (f32[4,3,4,16,127]{4,3,2,0,1:T(8,128)}, f32[4,3,4,16,127]{4,3,2,0,1:T(8,128)}, f32[4,3,4,16,127]{4,3,2,0,1:T(8,128)}, f32[4,3,4,16,127]{4,3,2,0,1:T(8,128)}) fusion(f32[4,6,4,16,128]{4,3,2,0,1:T(8,128)S(1)} %get-tuple-element.65, f32[4,3,4,16,128]{4,3,2,0,1:T(8,128)S(1)} %get-tuple-element.70), kind=kLoop, calls=%fused_computation.154 | loop fusion | bytes 3121152 | tf_op jit(solution)/shard_map/jvp()/slice | solution.py:38
  20.8 0.9 %fusion.39 = f32[4,1,4,16,128]{4,3,2,0,1:T(8,128)} fusion(f32[4,4,16,127]{3,2,1,0:T(8,128)S(1)} %get-tuple-element.76, f32[4,4,16,127]{3,2,1,0:T(8,128)S(1)} %get-tuple-element.75, f32[4,6,4,16,128]{4,3,2,0,1:T(8,128)S(1)} %get-tuple-element.65, f32[4,6,4,16,128]{4,3,2,1,0:T(8,128)S(1)} %copy-done), kind=kLoop, calls=%fused_computation.65 | loop fusion | flops 1835008 | bytes 1439744 | tf_op jit(solution)/shard_map/transpose(jvp())/broadcast_in_dim | solution.py:63
  21.9 9.8 %collective-permute-done.3 = f32[4,6,4,1,128]{4,3,2,0,1:T(1,128)} collective-permute-done((f32[4,6,4,1,128]{4,3,2,0,1:T(1,128)}, f32[4,6,4,1,128]{4,3,2,0,1:T(1,128)}, u32[]{:S(2)}, u32[]{:S(2)}) %collective-permute-start.3) | collective-permute-done | bytes 49184 | tf_op jit(solution)/shard_map/ppermute | solution.py:29
  31.7 8.6 %collective-permute-start = (f32[4,6,4,16,128]{4,3,2,1,0:T(8,128)}, f32[4,6,4,16,128]{4,3,2,1,0:T(8,128)}, u32[]{:S(2)}, u32[]{:S(2)}) collective-permute-start(f32[4,6,4,16,128]{4,3,2,1,0:T(8,128)} %param.8), channel_id=1, source_target_pairs={{2,0},{4,2},{6,4},{8,6},{10,8},{12,10},{14,12},{16,14},{18,16},{20... | collective-permute-start | bytes 2359304 | tf_op jit(solution)/shard_map/ppermute | solution.py:29
  40.4 2.7 %dynamic-update-slice.17 = f32[4,6,4,17,128]{4,3,2,0,1:T(8,128)} dynamic-update-slice(f32[4,6,4,17,128]{4,3,2,0,1:T(8,128)} %get-tuple-element.66, f32[4,6,4,1,128]{4,3,2,0,1:T(1,128)} %collective-permute-done.3, s32[]{} %constant.178, s32[]{} %constant.178, s32[]{} %constant.178, s32[]{} %constant.184, s32[]{} %constant.178) | dynamic-update-slice | bytes 98308 | tf_op jit(solution)/shard_map/concatenate | solution.py:25
  43.1 2.1 %add_add_fusion = (f32[4,3,4,16,128]{4,3,2,0,1:T(8,128)S(1)}, f32[4,3,4,16,128]{4,3,2,0,1:T(8,128)S(1)}) fusion(f32[4,3,4,16,128]{4,3,2,0,1:T(8,128)S(1)} %get-tuple-element.31, f32[4,3,4,16,127]{4,3,2,0,1:T(8,128)} %get-tuple-element.83, f32[4,3,4,16,127]{4,3,2,0,1:T(8,128)} %get-tuple-element.84, f32[4,3,4,128]{3,2,0,1:T(4,128)} %get-tuple-element.79, ...), kind=kLoop, calls=%fused_computation.37 | loop fusion | flops 2555904 | bytes 4411904 | tf_op jit(solution)/shard_map/transpose(jvp())/add_any | solution.py:59
  45.5 2.5 %collective-permute-start.4 = (f32[4,6,4,1,128]{4,3,2,0,1:T(1,128)S(1)}, f32[4,6,4,1,128]{4,3,2,0,1:T(1,128)S(1)}, u32[]{:S(2)}, u32[]{:S(2)}) collective-permute-start(f32[4,6,4,1,128]{4,3,2,0,1:T(1,128)S(1)} %get-tuple-element.45), channel_id=1, source_target_pairs={{0,1},{2,3},{4,5},{6,7},{8,9},{10,11},{12,13},{14,15},{16,17},{18,... | collective-permute-start | bytes 147464 | tf_op jit(solution)/shard_map/ppermute | solution.py:27
  51.4 1.8 %fusion.30 = f32[4,6,4,16,128]{4,3,2,1,0:T(8,128)} fusion(f32[4,6,4,16,128]{4,3,2,1,0:T(8,128)} %bitcast_dynamic-update-slice_fusion, f32[4,6,4,17,128]{4,3,2,0,1:T(8,128)} %dynamic-update-slice.17, f32[4,4,16,127]{3,2,1,0:T(8,128)S(1)} %copy-done.13, f32[4,4,16,127]{3,2,1,0:T(8,128)S(1)} %copy-done.12, f32[4,6,4,16,128]{4,3,2,0,1:T(8,128)S(1)} %get-tuple-element.65, ...), kind=kLoop, calls=%fused_computation.50 | loop fusion | flops 950272 | bytes 2015232 | tf_op jit(solution)/shard_map/jvp()/stack | solution.py:97
  53.7 1.3 %collective-permute-start.5 = (f32[4,6,4,1,128]{4,3,2,0,1:T(1,128)S(1)}, f32[4,6,4,1,128]{4,3,2,0,1:T(1,128)S(1)}, u32[]{:S(2)}, u32[]{:S(2)}) collective-permute-start(f32[4,6,4,1,128]{4,3,2,0,1:T(1,128)S(1)} %get-tuple-element.44), channel_id=1, source_target_pairs={{1,0},{3,2},{5,4},{7,6},{9,8},{11,10},{13,12},{15,14},{17,16},{19,... | collective-permute-start | bytes 147464 | tf_op jit(solution)/shard_map/ppermute | solution.py:29
  55.1 2.6 %scatter-add.6 = f32[4,6,4,16,128]{4,3,2,0,1:T(8,128)S(1)} dynamic-update-slice(f32[4,6,4,16,128]{4,3,2,0,1:T(8,128)S(1)} %slice.256, f32[4,6,4,1,128]{4,3,2,0,1:T(1,128)S(1)} %add_add_fusion.2, s32[]{:T(128)} %constant.110.clone.1, s32[]{:T(128)} %constant.110.clone.1, s32[]{:T(128)} %constant.110.clone.1, s32[]{:T(128)} %constant.110.clone.1, s32[]{:T(128)} %constant.110.clone.1) | dynamic-update-slice | bytes 98308 | tf_op jit(solution)/shard_map/scatter-add | solution.py:119
  57.7 2.0 %collective-permute-done.5 = f32[4,6,4,1,128]{4,3,2,0,1:T(1,128)S(1)} collective-permute-done((f32[4,6,4,1,128]{4,3,2,0,1:T(1,128)S(1)}, f32[4,6,4,1,128]{4,3,2,0,1:T(1,128)S(1)}, u32[]{:S(2)}, u32[]{:S(2)}) %collective-permute-start.5) | collective-permute-done | bytes 49184 | tf_op jit(solution)/shard_map/ppermute | solution.py:29
  59.7 2.6 %scatter-add.9 = f32[4,6,4,16,128]{4,3,2,0,1:T(8,128)S(1)} dynamic-update-slice(f32[4,6,4,16,128]{4,3,2,0,1:T(8,128)S(1)} %scatter-add.6, f32[4,6,4,1,128]{4,3,2,0,1:T(1,128)S(1)} %slice_add_fusion.2, s32[]{:T(128)} %constant.110.clone.1, s32[]{:T(128)} %constant.110.clone.1, s32[]{:T(128)} %constant.110.clone.1, s32[]{:T(128)} %constant.107.clone.1, s32[]{:T(128)} %constant.110.clone.1) | dynamic-update-slice | bytes 98308 | tf_op jit(solution)/shard_map/scatter-add | solution.py:120
  62.3 1.2 %constant_dynamic-update-slice_fusion.8 = f32[8,6,4,16,128]{4,3,2,1,0:T(8,128)S(1)} fusion(f32[4,6,4,16,128]{4,3,2,1,0:T(8,128)} %collective-permute-done.7), kind=kLoop, calls=%fused_computation.137 | loop fusion | bytes 1572864
  63.5 1.2 %constant_dynamic-update-slice_fusion.3 = f32[8,6,4,16,128]{4,3,2,1,0:T(8,128)S(1)} fusion(f32[4,6,4,16,128]{4,3,2,1,0:T(8,128)} %collective-permute-done.1), kind=kLoop, calls=%fused_computation.132 | loop fusion | bytes 1572864
  64.9 1.2 %constant_dynamic-update-slice_fusion.5 = f32[8,6,4,16,128]{4,3,2,1,0:T(8,128)S(1)} fusion(f32[8,6,4,16,128]{4,3,2,1,0:T(8,128)S(1)} %get-tuple-element.55, f32[4,6,4,16,128]{4,3,2,1,0:T(8,128)} %collective-permute-done.6), kind=kLoop, calls=%fused_computation.134 | loop fusion | bytes 1572864 | tf_op jit(solution)/shard_map/concatenate | solution.py:25
  66.1 1.3 %constant_dynamic-update-slice_fusion.1 = (f32[8,6,4,16,128]{4,3,2,1,0:T(8,128)S(1)}, f32[8,6,4,16,128]{4,3,2,1,0:T(8,128)S(1)}) fusion(f32[4,6,4,16,128]{4,3,2,1,0:T(8,128)} %param.8, f32[8,6,4,16,128]{4,3,2,1,0:T(8,128)S(1)} %constant_dynamic-update-slice_fusion.3), kind=kLoop, calls=%fused_computation.130 | loop fusion | bytes 2359296
  67.4 1.2 %constant_dynamic-update-slice_fusion = f32[8,6,4,16,128]{4,3,2,1,0:T(8,128)S(1)} fusion(f32[8,6,4,16,128]{4,3,2,1,0:T(8,128)S(1)} %get-tuple-element.57, f32[4,6,4,16,128]{4,3,2,1,0:T(8,128)} %collective-permute-done), kind=kLoop, calls=%fused_computation.129 | loop fusion | bytes 1572864 | tf_op jit(solution)/shard_map/concatenate | solution.py:25
  68.6 2.8 %fusion.5 = f32[4,6,4,16,128]{4,3,2,1,0:T(8,128)} fusion(f32[8,6,4,16,128]{4,3,2,1,0:T(8,128)S(1)} %get-tuple-element.56, f32[8,6,4,16,128]{4,3,2,1,0:T(8,128)S(1)} %constant_dynamic-update-slice_fusion.5, f32[4,6,4,16,128]{4,3,2,0,1:T(8,128)S(1)} %scatter-add.9, f32[4,6,4,16,128]{4,3,2,1,0:T(8,128)} %collective-permute-done.6, ...), kind=kLoop, calls=%fused_computation.10 | loop fusion | flops 2555904 | bytes 7864320 | tf_op jit(solution)/shard_map/sub | solution.py:121
  71.4 3.0 %fusion.13 = f32[4,6,4,16,128]{4,3,2,1,0:T(8,128)} fusion(f32[4,6,4,16,128]{4,3,2,1,0:T(8,128)} %fusion.30, f32[8,6,4,16,128]{4,3,2,1,0:T(8,128)S(1)} %get-tuple-element.58, f32[8,6,4,16,128]{4,3,2,1,0:T(8,128)S(1)} %constant_dynamic-update-slice_fusion, f32[4,6,4,16,128]{4,3,2,1,0:T(8,128)} %collective-permute-done, ...), kind=kLoop, calls=%fused_computation.21 | loop fusion | flops 2555904 | bytes 7864320 | tf_op jit(solution)/shard_map/add | solution.py:121
  (71 shorter events, 10.0 us)
Async XLA Ops:
  0.6 13.4 %copy-start = (f32[4,6,4,16,128]{4,3,2,1,0:T(8,128)S(1)}, f32[4,6,4,16,128]{4,3,2,1,0:T(8,128)}, u32[]{:S(2)}) copy-start(f32[4,6,4,16,128]{4,3,2,1,0:T(8,128)} %param.9) | copy-start | bytes 2359300
  0.6 61.7 %collective-permute-start.7 = (f32[4,6,4,16,128]{4,3,2,1,0:T(8,128)}, f32[4,6,4,16,128]{4,3,2,1,0:T(8,128)}, u32[]{:S(2)}, u32[]{:S(2)}) collective-permute-start(f32[4,6,4,16,128]{4,3,2,1,0:T(8,128)} %param.9), channel_id=1, source_target_pairs={{0,2},{2,4},{4,6},{6,8},{8,10},{10,12},{12,14},{14,16},{16,18},{18... | collective-permute-start | bytes 2359304 | tf_op jit(solution)/shard_map/ppermute | solution.py:27
  0.7 64.2 %collective-permute-start.6 = (f32[4,6,4,16,128]{4,3,2,1,0:T(8,128)}, f32[4,6,4,16,128]{4,3,2,1,0:T(8,128)}, u32[]{:S(2)}, u32[]{:S(2)}) collective-permute-start(f32[4,6,4,16,128]{4,3,2,1,0:T(8,128)} %param.9), channel_id=1, source_target_pairs={{2,0},{4,2},{6,4},{8,6},{10,8},{12,10},{14,12},{16,14},{18,16},{20... | collective-permute-start | bytes 2359304 | tf_op jit(solution)/shard_map/ppermute | solution.py:29
  4.0 59.5 %collective-permute-start.1 = (f32[4,6,4,16,128]{4,3,2,1,0:T(8,128)}, f32[4,6,4,16,128]{4,3,2,1,0:T(8,128)}, u32[]{:S(2)}, u32[]{:S(2)}) collective-permute-start(f32[4,6,4,16,128]{4,3,2,1,0:T(8,128)} %param.8), channel_id=1, source_target_pairs={{0,2},{2,4},{4,6},{6,8},{8,10},{10,12},{12,14},{14,16},{16,18},{18... | collective-permute-start | bytes 2359304 | tf_op jit(solution)/shard_map/ppermute | solution.py:27
  6.2 8.7 %copy-start.14 = (s32[4,4]{1,0:T(4,128)S(1)}, s32[4,4]{1,0:T(4,128)}, u32[]{:S(2)}) copy-start(s32[4,4]{1,0:T(4,128)} %param.11) | copy-start | bytes 196
  6.2 8.7 %copy-start.15 = (s32[4,4]{1,0:T(4,128)S(1)}, s32[4,4]{1,0:T(4,128)}, u32[]{:S(2)}) copy-start(s32[4,4]{1,0:T(4,128)} %param.10) | copy-start | bytes 196
  6.2 8.8 %copy-start.16 = (pred[3]{0:T(512)(128)(4,1)S(1)}, pred[3]{0:T(512)(128)(4,1)}, u32[]{:S(2)}) copy-start(pred[3]{0:T(512)(128)(4,1)} %constant.121.clone.1) | copy-start | bytes 13
  6.9 24.8 %collective-permute-start.3 = (f32[4,6,4,1,128]{4,3,2,0,1:T(1,128)}, f32[4,6,4,1,128]{4,3,2,0,1:T(1,128)}, u32[]{:S(2)}, u32[]{:S(2)}) collective-permute-start(f32[4,6,4,1,128]{4,3,2,0,1:T(1,128)} %get-tuple-element.62), channel_id=1, source_target_pairs={{1,0},{3,2},{5,4},{7,6},{9,8},{11,10},{13,12},{15,14},{17,16},{19,... | collective-permute-start | bytes 147464 | tf_op jit(solution)/shard_map/ppermute | solution.py:29
  8.2 34.8 %collective-permute-start.2 = (f32[4,6,4,1,128]{4,3,2,0,1:T(1,128)}, f32[4,6,4,1,128]{4,3,2,0,1:T(1,128)}, u32[]{:S(2)}, u32[]{:S(2)}) collective-permute-start(f32[4,6,4,1,128]{4,3,2,0,1:T(1,128)} %get-tuple-element.61), channel_id=1, source_target_pairs={{0,1},{2,3},{4,5},{6,7},{8,9},{10,11},{12,13},{14,15},{16,17},{18,... | collective-permute-start | bytes 147464 | tf_op jit(solution)/shard_map/ppermute | solution.py:27
  17.6 4.2 %copy-start.1 = (f32[4,1,4,16,128]{4,3,2,0,1:T(8,128)}, f32[4,1,4,16,128]{4,3,2,0,1:T(8,128)S(1)}, u32[]{:S(2)}) copy-start(f32[4,1,4,16,128]{4,3,2,0,1:T(8,128)S(1)} %get-tuple-element.35) | copy-start | bytes 393220
  18.4 3.4 %copy-start.9 = (f32[4,1,4,16,128]{4,3,2,0,1:T(8,128)S(1)}, f32[4,1,4,16,128]{4,3,2,0,1:T(8,128)}, u32[]{:S(2)}) copy-start(f32[4,1,4,16,128]{4,3,2,0,1:T(8,128)} %get-tuple-element.47) | copy-start | bytes 393220
  18.4 3.4 %copy-start.10 = (f32[4,1,4,16,128]{4,3,2,0,1:T(8,128)S(1)}, f32[4,1,4,16,128]{4,3,2,0,1:T(8,128)}, u32[]{:S(2)}) copy-start(f32[4,1,4,16,128]{4,3,2,0,1:T(8,128)} %get-tuple-element.48) | copy-start | bytes 393220
  31.7 35.7 %collective-permute-start = (f32[4,6,4,16,128]{4,3,2,1,0:T(8,128)}, f32[4,6,4,16,128]{4,3,2,1,0:T(8,128)}, u32[]{:S(2)}, u32[]{:S(2)}) collective-permute-start(f32[4,6,4,16,128]{4,3,2,1,0:T(8,128)} %param.8), channel_id=1, source_target_pairs={{2,0},{4,2},{6,4},{8,6},{10,8},{12,10},{14,12},{16,14},{18,16},{20... | collective-permute-start | bytes 2359304 | tf_op jit(solution)/shard_map/ppermute | solution.py:29
  43.0 2.2 %copy-start.4 = (f32[4,1,4,16,128]{4,3,2,0,1:T(8,128)S(1)}, f32[4,1,4,16,128]{4,3,2,0,1:T(8,128)}, u32[]{:S(2)}) copy-start(f32[4,1,4,16,128]{4,3,2,0,1:T(8,128)} %get-tuple-element.46) | copy-start | bytes 393220
  43.1 2.2 %copy-start.5 = (f32[4,1,4,16,128]{4,3,2,0,1:T(8,128)S(1)}, f32[4,1,4,16,128]{4,3,2,0,1:T(8,128)}, u32[]{:S(2)}) copy-start(f32[4,1,4,16,128]{4,3,2,0,1:T(8,128)} %get-tuple-element.34) | copy-start | bytes 393220
  43.1 2.2 %copy-start.6 = (f32[4,1,4,16,128]{4,3,2,0,1:T(8,128)S(1)}, f32[4,1,4,16,128]{4,3,2,0,1:T(8,128)}, u32[]{:S(2)}) copy-start(f32[4,1,4,16,128]{4,3,2,0,1:T(8,128)} %get-tuple-element.53) | copy-start | bytes 393220
  43.1 2.2 %copy-start.7 = (f32[4,1,4,16,128]{4,3,2,0,1:T(8,128)S(1)}, f32[4,1,4,16,128]{4,3,2,0,1:T(8,128)}, u32[]{:S(2)}) copy-start(f32[4,1,4,16,128]{4,3,2,0,1:T(8,128)} %get-tuple-element.49) | copy-start | bytes 393220
  43.1 2.2 %copy-start.8 = (f32[4,1,4,16,128]{4,3,2,0,1:T(8,128)S(1)}, f32[4,1,4,16,128]{4,3,2,0,1:T(8,128)}, u32[]{:S(2)}) copy-start(f32[4,1,4,16,128]{4,3,2,0,1:T(8,128)} %get-tuple-element.51) | copy-start | bytes 393220
  43.1 2.2 %copy-start.11 = (f32[4,1,4,16,128]{4,3,2,0,1:T(8,128)S(1)}, f32[4,1,4,16,128]{4,3,2,0,1:T(8,128)}, u32[]{:S(2)}) copy-start(f32[4,1,4,16,128]{4,3,2,0,1:T(8,128)} %fusion.39) | copy-start | bytes 393220
  45.4 2.6 %copy-start.2 = (f32[4,1,4,16,128]{4,3,2,0,1:T(8,128)S(1)}, f32[4,1,4,16,128]{4,3,2,0,1:T(8,128)}, u32[]{:S(2)}) copy-start(f32[4,1,4,16,128]{4,3,2,0,1:T(8,128)} %copy-done.1) | copy-start | bytes 393220
  45.5 6.0 %copy-start.12 = (f32[4,4,16,127]{3,2,1,0:T(8,128)S(1)}, f32[4,4,16,127]{3,2,1,0:T(8,128)}, u32[]{:S(2)}) copy-start(f32[4,4,16,127]{3,2,1,0:T(8,128)} %get-tuple-element.77) | copy-start | bytes 390148
  45.5 5.9 %copy-start.13 = (f32[4,4,16,127]{3,2,1,0:T(8,128)S(1)}, f32[4,4,16,127]{3,2,1,0:T(8,128)}, u32[]{:S(2)}) copy-start(f32[4,4,16,127]{3,2,1,0:T(8,128)} %get-tuple-element.78) | copy-start | bytes 390148
  45.5 8.2 %collective-permute-start.4 = (f32[4,6,4,1,128]{4,3,2,0,1:T(1,128)S(1)}, f32[4,6,4,1,128]{4,3,2,0,1:T(1,128)S(1)}, u32[]{:S(2)}, u32[]{:S(2)}) collective-permute-start(f32[4,6,4,1,128]{4,3,2,0,1:T(1,128)S(1)} %get-tuple-element.45), channel_id=1, source_target_pairs={{0,1},{2,3},{4,5},{6,7},{8,9},{10,11},{12,13},{14,15},{16,17},{18,... | collective-permute-start | bytes 147464 | tf_op jit(solution)/shard_map/ppermute | solution.py:27
  53.7 6.0 %collective-permute-start.5 = (f32[4,6,4,1,128]{4,3,2,0,1:T(1,128)S(1)}, f32[4,6,4,1,128]{4,3,2,0,1:T(1,128)S(1)}, u32[]{:S(2)}, u32[]{:S(2)}) collective-permute-start(f32[4,6,4,1,128]{4,3,2,0,1:T(1,128)S(1)} %get-tuple-element.44), channel_id=1, source_target_pairs={{1,0},{3,2},{5,4},{7,6},{9,8},{11,10},{13,12},{15,14},{17,16},{19,... | collective-permute-start | bytes 147464 | tf_op jit(solution)/shard_map/ppermute | solution.py:29
  (1 other events, 2.2 us)
where the time goes:
time: 74.9 us; the launch traced here: 74.4 us
  starting transfers between devices  22.8 us (30%)
  local copies, waits for them, and re-layouts  20.1 us (27%)
  other arithmetic  18.7 us (25%)
  waiting for transfers between devices  11.9 us (16%)
  between operations  1.02 us (1%)
    ppermute x4, starting transfers between devices, extended_2(): lax.ppermute(head, axis, [((i + 1) % count, i) for i in range(ends)])  14.5 us
    ppermute x4, waiting for transfers between devices, extended_2(): lax.ppermute(head, axis, [((i + 1) % count, i) for i in range(ends)])  11.8 us
    ppermute x4, starting transfers between devices, extended_2(): lax.ppermute(tail, axis, [(i, (i + 1) % count) for i in range(ends)])  8.32 us
    unnamed x41, local copies, waits for them, and re-layouts  6.85 us
    concatenate x3, local copies, waits for them, and re-layouts, extended_2(): jnp.concatenate([lax.ppermute(tail, axis, [(i, (i + 1) % count) for i in...  5.03 us
    add x1, other arithmetic, local(): return (state_time + forward, local_adj - adjoint_time)  3.02 us
    sub x1, other arithmetic, local(): return (state_time + forward, local_adj - adjoint_time)  2.79 us
    unnamed x4, other arithmetic  2.76 us
  transfers between devices with their start and end apart: 8, of which 2 were waited for; matrix products, arithmetic and copies ran while one was open for 43% of the time, Pallas kernels for 0%

commit v1 on v0

v1 whole, which is shorter than its diff:
```python
import jax
import jax.numpy as jnp
from jax import lax
from jax.experimental import pallas as pl
from jax.experimental.pallas import tpu as pltpu
from jax.sharding import PartitionSpec as P

STENCIL = (0.8, -0.2, 4.0 / 105.0, -1.0 / 280.0)
TIME_SCALE = 4.0
FLOW_VELOCITY = 1.0
AXIAL_DISPERSION = 0.3
RADIAL_SPREADING = 0.2
BINDING_STRENGTH = (1.5, 0.6)
HEAT_EXPONENT = (0.5, 0.3)
KINETIC = (1.2, 0.7)
CAPACITY = (2.0, 1.0)
SORPTION_HEAT = (0.4, 0.25)
PURGE_GAIN = 1.5

MESH = pl.DeviceIdType.MESH


def _kernel(n_tm, tbl, st, ad, res, adj, rl_st, rr_st, rl_ad, rr_ad, h_st, h_ad, send, recv):
    inst, comp, beds, nz, nr = st.shape
    me = lax.axis_index("tm")
    sec = lax.axis_index("sec")
    right = lax.rem(me + 1, n_tm)
    left = lax.rem(me + n_tm - 1, n_tm)
    partner = 1 - sec

    barrier = pltpu.get_barrier_semaphore()
    for dev in ((left, sec), (right, sec), (me, partner)):
        pl.semaphore_signal(barrier, inc=1, device_id=dev, device_id_type=MESH)
    pl.semaphore_wait(barrier, 3)

    row_src = (nz - 1) * (1 - sec)
    halo_copies = []
    for i, (src, dst) in enumerate(((st, h_st), (ad, h_ad))):
        cp = pltpu.make_async_remote_copy(
            src_ref=src.at[:, :, :, pl.ds(row_src, 1), :],
            dst_ref=dst.at[:, :, :, pl.ds(0, 1), :],
            send_sem=send.at[4 + i],
            recv_sem=recv.at[4 + i],
            device_id=(me, partner),
            device_id_type=MESH,
        )
        cp.start()
        halo_copies.append(cp)
    big = []
    for i, (src, dst, dev) in enumerate(
        ((st, rl_st, right), (st, rr_st, left), (ad, rl_ad, right), (ad, rr_ad, left))
    ):
        cp = pltpu.make_async_remote_copy(
            src_ref=src,
            dst_ref=dst,
            send_sem=send.at[i],
            recv_sem=recv.at[i],
            device_id=(dev, sec),
            device_id_type=MESH,
        )
        cp.start()
        big.append(cp)

    for cp in halo_copies:
        cp.wait()

    sec_f = sec.astype(jnp.float32)
    row = lax.broadcasted_iota(jnp.int32, (nz, nr), 0)
    lane = lax.broadcasted_iota(jnp.int32, (nz, nr), 1)
    first_row = row == 0
    last_row = row == nz - 1
    first_lane = lane == 0
    last_lane = lane == nr - 1

    def radial(x):
        lower = jnp.where(first_lane, 0.0, pltpu.roll(x, 1, 1))
        upper = jnp.where(last_lane, 0.0, pltpu.roll(x, nr - 1, 1))
        return upper - 2.0 * x + lower

    def axial(x, below, above):
        zm = jnp.where(first_row, below, pltpu.roll(x, 1, 0))
        zp = jnp.where(last_row, above, pltpu.roll(x, nz - 1, 0))
        return zm, zp

    def transport(x, below, above):
        zm, zp = axial(x, below, above)
        out = FLOW_VELOCITY * (x - zm) - AXIAL_DISPERSION * (zp - 2.0 * x + zm)
        return out - RADIAL_SPREADING * radial(x)

    def transport_t(lam, below, above):
        lm, lp = axial(lam, below, above)
        out = FLOW_VELOCITY * (lam - lp) - AXIAL_DISPERSION * (lm - 2.0 * lam + lp)
        return out - RADIAL_SPREADING * radial(lam)

    def spatial_body(t, carry):
        for b in range(beds):
            x = [st[t, c, b] for c in range(comp)]
            lam = [ad[t, c, b] for c in range(comp)]
            hs = [h_st[t, c, b, 0:1, :] for c in range(comp)]
            ha = [h_ad[t, c, b, 0:1, :] for c in range(comp)]
            y1, y2, y3, q1, q2, temp = x
            b1 = BINDING_STRENGTH[0] * jnp.exp(HEAT_EXPONENT[0] * temp)
            b2 = BINDING_STRENGTH[1] * jnp.exp(HEAT_EXPONENT[1] * temp)
            den = 1.0 + b1 * y1 + b2 * y2
            p1 = b1 * y1 / den
            p2 = b2 * y2 / den
            rate1 = KINETIC[0] * (CAPACITY[0] * p1 - q1)
            rate2 = KINETIC[1] * (CAPACITY[1] * p2 - q2)
            tr = {}
            trt = {}
            for c in (0, 1, 2, 5):
                below = hs[c] * sec_f
                above = hs[c] * (1.0 - sec_f)
                tr[c] = transport(x[c], below, above)
                lbelow = ha[c] * sec_f
                labove = ha[c] * (1.0 - sec_f)
                trt[c] = transport_t(lam[c], lbelow, labove)
            res[t, 0, b] = tr[0] + rate1
            res[t, 1, b] = tr[1] + rate2
            res[t, 2, b] = tr[2]
            res[t, 3, b] = -rate1
            res[t, 4, b] = -rate2
            res[t, 5, b] = tr[5] - (SORPTION_HEAT[0] * rate1 + SORPTION_HEAT[1] * rate2)
            mu1 = lam[0] - lam[3] - SORPTION_HEAT[0] * lam[5]
            mu2 = lam[1] - lam[4] - SORPTION_HEAT[1] * lam[5]
            n1 = (KINETIC[0] * CAPACITY[0]) * mu1
            n2 = (KINETIC[1] * CAPACITY[1]) * mu2
            cden = -(n1 * p1 + n2 * p2) / den
            cu1 = n1 / den + cden
            cu2 = n2 / den + cden
            adj[t, 0, b] = trt[0] + b1 * cu1
            adj[t, 1, b] = trt[1] + b2 * cu2
            adj[t, 2, b] = trt[2]
            adj[t, 3, b] = -KINETIC[0] * mu1
            adj[t, 4, b] = -KINETIC[1] * mu2
            adj[t, 5, b] = trt[5] + (HEAT_EXPONENT[0] * y1 * b1 * cu1 + HEAT_EXPONENT[1] * y2 * b2 * cu2)
        return carry

    lax.fori_loop(0, inst, spatial_body, 0)

    @pl.when(sec == 1)
    def _():
        def purge_body(t, carry):
            base = t * (beds * beds)
            for c in range(3):
                ys = [st[t, c, b, nz - 1 : nz, :] for b in range(beds)]
                ls = [ad[t, c, b, nz - 1 : nz, :] for b in range(beds)]
                for b in range(beds):
                    gain = tbl[beds * beds * inst + t * beds + b]
                    inc = tbl[base + b * beds] * ys[0]
                    for bp in range(1, beds):
                        inc = inc + tbl[base + b * beds + bp] * ys[bp]
                    res[t, c, b, nz - 1 : nz, :] = res[t, c, b, nz - 1 : nz, :] + gain * (ys[b] - inc)
                    back = gain * ls[b]
                    for bb in range(beds):
                        w = tbl[base + bb * beds + b] * tbl[beds * beds * inst + t * beds + bb]
                        back = back - w * ls[bb]
                    adj[t, c, b, nz - 1 : nz, :] = adj[t, c, b, nz - 1 : nz, :] + back
            return carry

        lax.fori_loop(0, inst, purge_body, 0)

    for cp in big:
        cp.wait()

    def pick(own, lft, rgt, j, c):
        if j < 0:
            return lft[j + inst, c]
        if j >= inst:
            return rgt[j - inst, c]
        return own[j, c]

    def time_body(c, carry):
        for t in range(inst):
            acc_s = None
            acc_a = None
            for k, w in enumerate(STENCIL):
                s = k + 1
                ds = w * (pick(st, rl_st, rr_st, t + s, c) - pick(st, rl_st, rr_st, t - s, c))
                da = w * (pick(ad, rl_ad, rr_ad, t + s, c) - pick(ad, rl_ad, rr_ad, t - s, c))
                acc_s = ds if acc_s is None else acc_s + ds
                acc_a = da if acc_a is None else acc_a + da
            res[t, c] = TIME_SCALE * acc_s + res[t, c]
            adj[t, c] = adj[t, c] - TIME_SCALE * acc_a
        return carry

    lax.fori_loop(0, comp, time_body, 0)


def local(state, adjoint, plan, valve):
    n_tm = lax.axis_size("tm")
    inst, comp, beds, nz, nr = state.shape
    bed_ids = jnp.arange(beds, dtype=jnp.int32)
    source = (bed_ids[None, :] + plan) % beds
    onehot = (source[:, :, None] == bed_ids[None, None, :]).astype(jnp.float32)
    gain = PURGE_GAIN * valve.astype(jnp.float32)
    tbl = jnp.concatenate([onehot.reshape(-1), gain.reshape(-1)])
    block = jax.ShapeDtypeStruct(state.shape, jnp.float32)
    vmem = pl.BlockSpec(memory_space=pltpu.VMEM)
    halo_shape = (inst, comp, beds, 8, nr)

    def kern(*refs):
        _kernel(n_tm, *refs)

    res, adj = pl.pallas_call(
        kern,
        out_shape=(block, block),
        in_specs=[pl.BlockSpec(memory_space=pltpu.SMEM), vmem, vmem],
        out_specs=(vmem, vmem),
        scratch_shapes=[pltpu.VMEM(state.shape, jnp.float32)] * 4
        + [pltpu.VMEM(halo_shape, jnp.float32)] * 2
        + [pltpu.SemaphoreType.DMA((6,)), pltpu.SemaphoreType.DMA((6,))],
        compiler_params=pltpu.CompilerParams(collective_id=0, has_side_effects=True),
    )(tbl, state, adjoint)
    return res, adj


def solution(mesh):
    return jax.shard_map(
        local,
        mesh=mesh,
        in_specs=(
            P("tm", None, None, "sec", None),
            P("tm", None, None, "sec", None),
            P("tm", None),
            P("tm", None),
        ),
        out_specs=(P("tm", None, None, "sec", None), P("tm", None, None, "sec", None)),
        check_vma=False,
    )
```

time: 74.9 us -> 50.8 us (0.68)
  the two profiles are of different devices: /device:TPU:18 before, /device:TPU:1 now
where the time goes in v1:
time: 50.8 us; the launch traced here: 50.7 us
  Pallas kernels  45.4 us (89%)
  local copies, waits for them, and re-layouts  3.23 us (6%)
  other arithmetic  1.36 us (3%)
  between operations  0.67 us (1%)
    pallas_call x1, Pallas kernels, local(): pl.pallas_call(kern, out_shape=(block, block), in_specs=[pl.BlockSpec(mem...  45.4 us
    unnamed x6, local copies, waits for them, and re-layouts  3.05 us

profile of v1, /device:TPU:1, one launch (start us, length us, event | category | flops | bytes accessed | tf_op | source)
XLA Modules:
  0.0 50.7 jit_solution(7784804542127117188)
XLA Ops:
  0.6 0.0 copy-start.1
  0.6 0.7 %add_select_fusion = s32[4,4]{1,0:T(4,128)S(1)} fusion(s32[4,4]{1,0:T(4,128)} %param.6), kind=kLoop, calls=%fused_computation.2 | loop fusion | flops 192 | bytes 128 | tf_op jit(solution)/shard_map/jit(remainder)/select_n | solution.py:194
  1.3 0.0 copy-done.1
  1.4 0.1 reshape.14
  1.4 0.1 fusion
  1.5 0.1 reshape.15
  1.6 0.6 %pad_maximum_fusion.refs_0_ = f32[80]{0:T(128)} fusion(f32[16]{0:T(128)S(1)} %reshape.14, f32[64]{0:T(128)S(1)} %reshape.15), kind=kLoop, calls=%fused_computation.7 | loop fusion | flops 80 | bytes 640 | tf_op jit(solution)/shard_map/concatenate | solution.py:197
  2.2 45.4 %shard_map.59 = (f32[4,6,4,16,128]{4,3,2,1,0:T(8,128)}, f32[4,6,4,16,128]{4,3,2,1,0:T(8,128)}) custom-call(f32[80]{0:T(128)} %pad_maximum_fusion.refs_0_, f32[4,6,4,16,128]{4,3,2,1,0:T(8,128)} %refs_1_.1, f32[4,6,4,16,128]{4,3,2,1,0:T(8,128)} %refs_2_.1), custom_call_target="tpu_custom_call" | custom-call | tf_op jit(solution)/shard_map/pallas_call | solution.py:205
  47.6 0.0 copy-start
  47.6 2.2 %copy.8 = f32[4,6,4,16,128]{4,3,2,1,0:T(8,128)} copy(f32[4,6,4,16,128]{4,3,2,1,0:T(8,128)} %get-tuple-element.4) | data formatting | bytes 1572864
  49.8 0.0 copy-done
  49.8 0.9 %copy.9 = f32[4,6,4,16,128]{4,3,2,1,0:T(8,128)} copy(f32[4,6,4,16,128]{4,3,2,1,0:T(8,128)S(1)} %copy-done) | data formatting | bytes 1572864
  (1 shorter events, 0.0 us)
Async XLA Ops:
  0.6 0.7 %copy-start.1 = (s32[4,4]{1,0:T(4,128)S(1)}, s32[4,4]{1,0:T(4,128)}, u32[]{:S(2)}) copy-start(s32[4,4]{1,0:T(4,128)} %param.7) | copy-start | bytes 196
  47.6 2.2 %copy-start = (f32[4,6,4,16,128]{4,3,2,1,0:T(8,128)S(1)}, f32[4,6,4,16,128]{4,3,2,1,0:T(8,128)}, u32[]{:S(2)}) copy-start(f32[4,6,4,16,128]{4,3,2,1,0:T(8,128)} %get-tuple-element.5) | copy-start | bytes 2359300

commit v2 on v1

--- a/solution.py
+++ b/solution.py
@@ -20,46 +20,66 @@
 MESH = pl.DeviceIdType.MESH
 
 
-def _kernel(n_tm, tbl, st, ad, res, adj, rl_st, rr_st, rl_ad, rr_ad, h_st, h_ad, send, recv):
+def _kernel(n_tm, tbl, st, ad, res, adj, rv_st, rv_ad, ry_st, ry_ad, h_st, h_ad, send, recv):
     inst, comp, beds, nz, nr = st.shape
     me = lax.axis_index("tm")
     sec = lax.axis_index("sec")
-    right = lax.rem(me + 1, n_tm)
-    left = lax.rem(me + n_tm - 1, n_tm)
-    partner = 1 - sec
+    core = lax.rem(me, 2)
+    ring = lax.div(me, 4)
+    y = lax.rem(lax.div(me, 2), 2) * 2 + sec
+
+    def at(yy, cc):
+        return (ring * 4 + lax.div(yy, 2) * 2 + cc, lax.rem(yy, 2))
+
+    def up_of(dev):
+        t, s = dev
+        yy = lax.rem(lax.div(t, 2), 2) * 2 + s
+        yy = lax.rem(yy + 1, 4)
+        return (lax.div(t, 4) * 4 + lax.div(yy, 2) * 2 + lax.rem(t, 2), lax.rem(yy, 2))
+
+    def dn_of(dev):
+        t, s = dev
+        yy = lax.rem(lax.div(t, 2), 2) * 2 + s
+        yy = lax.rem(yy + 3, 4)
+        return (lax.div(t, 4) * 4 + lax.div(yy, 2) * 2 + lax.rem(t, 2), lax.rem(yy, 2))
+
+    def cross_of(dev):
+        t, s = dev
+        return (lax.rem(t + 2 * lax.rem(t, 2) - 1 + n_tm, n_tm), s)
+
+    mine = (me, sec)
+    pair = (me + 1 - 2 * core, sec)
+    up = at(lax.rem(y + 1, 4), core)
+    dn = at(lax.rem(y + 3, 4), core)
+    fwd_st = cross_of(dn)
+    fwd_ad = cross_of(up)
+    cross = cross_of(mine)
+    from_st = up_of(cross)
+    from_ad = dn_of(cross)
+    partner = (me, 1 - sec)
 
     barrier = pltpu.get_barrier_semaphore()
-    for dev in ((left, sec), (right, sec), (me, partner)):
+    for dev in (pair, up, dn, fwd_st, fwd_ad, from_st, from_ad):
         pl.semaphore_signal(barrier, inc=1, device_id=dev, device_id_type=MESH)
-    pl.semaphore_wait(barrier, 3)
-
-    row_src = (nz - 1) * (1 - sec)
-    halo_copies = []
-    for i, (src, dst) in enumerate(((st, h_st), (ad, h_ad))):
+    pl.semaphore_wait(barrier, 7)
+
+    def rcopy(src, dst, i, dev):
         cp = pltpu.make_async_remote_copy(
-            src_ref=src.at[:, :, :, pl.ds(row_src, 1), :],
-            dst_ref=dst.at[:, :, :, pl.ds(0, 1), :],
-            send_sem=send.at[4 + i],
-            recv_sem=recv.at[4 + i],
-            device_id=(me, partner),
-            device_id_type=MESH,
+            src_ref=src, dst_ref=dst, send_sem=send.at[i], recv_sem=recv.at[i],
+            device_id=dev, device_id_type=MESH,
         )
         cp.start()
-        halo_copies.append(cp)
-    big = []
-    for i, (src, dst, dev) in enumerate(
-        ((st, rl_st, right), (st, rr_st, left), (ad, rl_ad, right), (ad, rr_ad, left))
-    ):
-        cp = pltpu.make_async_remote_copy(
-            src_ref=src,
-            dst_ref=dst,
-            send_sem=send.at[i],
-            recv_sem=recv.at[i],
-            device_id=(dev, sec),
-            device_id_type=MESH,
-        )
-        cp.start()
-        big.append(cp)
+        return cp
+
+    row_src = (nz - 1) * (1 - sec)
+    halo_copies = [
+        rcopy(src.at[:, :, :, pl.ds(row_src, 1), :], dst.at[:, :, :, pl.ds(0, 1), :], 4 + i, partner)
+        for i, (src, dst) in enumerate(((st, h_st), (ad, h_ad)))
+    ]
+    leg_st = rcopy(st, ry_st, 0, up)
+    leg_ad = rcopy(ad, ry_ad, 1, dn)
+    near_st = rcopy(st, rv_st.at[core], 2, pair)
+    near_ad = rcopy(ad, rv_ad.at[core], 3, pair)
 
     for cp in halo_copies:
         cp.wait()
@@ -160,14 +180,18 @@
 
         lax.fori_loop(0, inst, purge_body, 0)
 
-    for cp in big:
-        cp.wait()
-
-    def pick(own, lft, rgt, j, c):
+    leg_st.wait_recv()
+    on_st = rcopy(ry_st, rv_st.at[1 - core], 6, fwd_st)
+    leg_ad.wait_recv()
+    on_ad = rcopy(ry_ad, rv_ad.at[1 - core], 7, fwd_ad)
+    for cp in (near_st, near_ad, on_st, on_ad):
+        cp.wait_recv()
+
+    def pick(own, recvd, j, c):
         if j < 0:
-            return lft[j + inst, c]
+            return recvd[0, j + inst, c]
         if j >= inst:
-            return rgt[j - inst, c]
+            return recvd[1, j - inst, c]
         return own[j, c]
 
     def time_body(c, carry):
@@ -176,8 +200,8 @@
             acc_a = None
             for k, w in enumerate(STENCIL):
                 s = k + 1
-                ds = w * (pick(st, rl_st, rr_st, t + s, c) - pick(st, rl_st, rr_st, t - s, c))
-                da = w * (pick(ad, rl_ad, rr_ad, t + s, c) - pick(ad, rl_ad, rr_ad, t - s, c))
+                ds = w * (pick(st, rv_st, t + s, c) - pick(st, rv_st, t - s, c))
+                da = w * (pick(ad, rv_ad, t + s, c) - pick(ad, rv_ad, t - s, c))
                 acc_s = ds if acc_s is None else acc_s + ds
                 acc_a = da if acc_a is None else acc_a + da
             res[t, c] = TIME_SCALE * acc_s + res[t, c]
@@ -185,6 +209,8 @@
         return carry
 
     lax.fori_loop(0, comp, time_body, 0)
+    for cp in (leg_st, leg_ad, near_st, near_ad, on_st, on_ad):
+        cp.wait_send()
 
 
 def local(state, adjoint, plan, valve):
@@ -207,9 +233,10 @@
         out_shape=(block, block),
         in_specs=[pl.BlockSpec(memory_space=pltpu.SMEM), vmem, vmem],
         out_specs=(vmem, vmem),
-        scratch_shapes=[pltpu.VMEM(state.shape, jnp.float32)] * 4
+        scratch_shapes=[pltpu.VMEM((2,) + state.shape, jnp.float32)] * 2
+        + [pltpu.VMEM(state.shape, jnp.float32)] * 2
         + [pltpu.VMEM(halo_shape, jnp.float32)] * 2
-        + [pltpu.SemaphoreType.DMA((6,)), pltpu.SemaphoreType.DMA((6,))],
+        + [pltpu.SemaphoreType.DMA((8,)), pltpu.SemaphoreType.DMA((8,))],
         compiler_params=pltpu.CompilerParams(collective_id=0, has_side_effects=True),
     )(tbl, state, adjoint)
     return res, adj

time: 50.8 us -> 60.7 us (1.19)
  Pallas kernels: 45.4 us -> 55.2 us
    pallas_call x1, Pallas kernels: 45.4 us -> 55.2 us  [local(): pl.pallas_call(kern, out_shape=(block, block), in_specs=[pl.BlockSpec(mem...]
where the time goes in v2:
time: 60.7 us; the launch traced here: 60.5 us
  Pallas kernels  55.2 us (91%)
  local copies, waits for them, and re-layouts  3.23 us (5%)
  other arithmetic  1.36 us (2%)
  between operations  0.67 us (1%)
    pallas_call x1, Pallas kernels, local(): pl.pallas_call(kern, out_shape=(block, block), in_specs=[pl.BlockSpec(mem...  55.2 us
    unnamed x6, local copies, waits for them, and re-layouts  3.05 us

profile of v2, /device:TPU:1, one launch (start us, length us, event | category | flops | bytes accessed | tf_op | source)
XLA Modules:
  0.0 60.5 jit_solution(17605590224607454998)
XLA Ops:
  0.6 0.0 copy-start.1
  0.6 0.7 %add_select_fusion = s32[4,4]{1,0:T(4,128)S(1)} fusion(s32[4,4]{1,0:T(4,128)} %param.6), kind=kLoop, calls=%fused_computation.2 | loop fusion | flops 192 | bytes 128 | tf_op jit(solution)/shard_map/jit(remainder)/select_n | solution.py:220
  1.3 0.0 copy-done.1
  1.4 0.1 reshape.14
  1.4 0.1 fusion
  1.5 0.1 reshape.15
  1.6 0.6 pad_maximum_fusion.refs_0_
  2.2 55.2 %shard_map.59 = (f32[4,6,4,16,128]{4,3,2,1,0:T(8,128)}, f32[4,6,4,16,128]{4,3,2,1,0:T(8,128)}) custom-call(f32[80]{0:T(128)} %pad_maximum_fusion.refs_0_, f32[4,6,4,16,128]{4,3,2,1,0:T(8,128)} %refs_1_.1, f32[4,6,4,16,128]{4,3,2,1,0:T(8,128)} %refs_2_.1), custom_call_target="tpu_custom_call" | custom-call | tf_op jit(solution)/shard_map/pallas_call | solution.py:231
  57.4 0.0 copy-start
  57.5 2.2 %copy.8 = f32[4,6,4,16,128]{4,3,2,1,0:T(8,128)} copy(f32[4,6,4,16,128]{4,3,2,1,0:T(8,128)} %get-tuple-element.4) | data formatting | bytes 1572864
  59.6 0.0 copy-done
  59.6 0.9 %copy.9 = f32[4,6,4,16,128]{4,3,2,1,0:T(8,128)} copy(f32[4,6,4,16,128]{4,3,2,1,0:T(8,128)S(1)} %copy-done) | data formatting | bytes 1572864
  (1 shorter events, 0.0 us)
Async XLA Ops:
  0.6 0.7 %copy-start.1 = (s32[4,4]{1,0:T(4,128)S(1)}, s32[4,4]{1,0:T(4,128)}, u32[]{:S(2)}) copy-start(s32[4,4]{1,0:T(4,128)} %param.7) | copy-start | bytes 196
  57.4 2.2 %copy-start = (f32[4,6,4,16,128]{4,3,2,1,0:T(8,128)S(1)}, f32[4,6,4,16,128]{4,3,2,1,0:T(8,128)}, u32[]{:S(2)}) copy-start(f32[4,6,4,16,128]{4,3,2,1,0:T(8,128)} %get-tuple-element.5) | copy-start | bytes 2359300

commit v3 on v2

--- a/solution.py
+++ b/solution.py
@@ -20,48 +20,19 @@
 MESH = pl.DeviceIdType.MESH
 
 
-def _kernel(n_tm, tbl, st, ad, res, adj, rv_st, rv_ad, ry_st, ry_ad, h_st, h_ad, send, recv):
+def _kernel(n_tm, plan, valve, st, ad, res, adj, rv_st, rv_ad, h_st, h_ad, send, recv):
     inst, comp, beds, nz, nr = st.shape
     me = lax.axis_index("tm")
     sec = lax.axis_index("sec")
     core = lax.rem(me, 2)
-    ring = lax.div(me, 4)
-    y = lax.rem(lax.div(me, 2), 2) * 2 + sec
-
-    def at(yy, cc):
-        return (ring * 4 + lax.div(yy, 2) * 2 + cc, lax.rem(yy, 2))
-
-    def up_of(dev):
-        t, s = dev
-        yy = lax.rem(lax.div(t, 2), 2) * 2 + s
-        yy = lax.rem(yy + 1, 4)
-        return (lax.div(t, 4) * 4 + lax.div(yy, 2) * 2 + lax.rem(t, 2), lax.rem(yy, 2))
-
-    def dn_of(dev):
-        t, s = dev
-        yy = lax.rem(lax.div(t, 2), 2) * 2 + s
-        yy = lax.rem(yy + 3, 4)
-        return (lax.div(t, 4) * 4 + lax.div(yy, 2) * 2 + lax.rem(t, 2), lax.rem(yy, 2))
-
-    def cross_of(dev):
-        t, s = dev
-        return (lax.rem(t + 2 * lax.rem(t, 2) - 1 + n_tm, n_tm), s)
-
-    mine = (me, sec)
     pair = (me + 1 - 2 * core, sec)
-    up = at(lax.rem(y + 1, 4), core)
-    dn = at(lax.rem(y + 3, 4), core)
-    fwd_st = cross_of(dn)
-    fwd_ad = cross_of(up)
-    cross = cross_of(mine)
-    from_st = up_of(cross)
-    from_ad = dn_of(cross)
+    cross = (lax.rem(me + 2 * core - 1 + n_tm, n_tm), sec)
     partner = (me, 1 - sec)
 
     barrier = pltpu.get_barrier_semaphore()
-    for dev in (pair, up, dn, fwd_st, fwd_ad, from_st, from_ad):
+    for dev in (pair, cross, partner):
         pl.semaphore_signal(barrier, inc=1, device_id=dev, device_id_type=MESH)
-    pl.semaphore_wait(barrier, 7)
+    pl.semaphore_wait(barrier, 3)
 
     def rcopy(src, dst, i, dev):
         cp = pltpu.make_async_remote_copy(
@@ -76,13 +47,13 @@
         rcopy(src.at[:, :, :, pl.ds(row_src, 1), :], dst.at[:, :, :, pl.ds(0, 1), :], 4 + i, partner)
         for i, (src, dst) in enumerate(((st, h_st), (ad, h_ad)))
     ]
-    leg_st = rcopy(st, ry_st, 0, up)
-    leg_ad = rcopy(ad, ry_ad, 1, dn)
+    far_st = rcopy(st, rv_st.at[1 - core], 0, cross)
+    far_ad = rcopy(ad, rv_ad.at[1 - core], 1, cross)
     near_st = rcopy(st, rv_st.at[core], 2, pair)
     near_ad = rcopy(ad, rv_ad.at[core], 3, pair)
 
     for cp in halo_copies:
-        cp.wait()
+        cp.wait_recv()
 
     sec_f = sec.astype(jnp.float32)
     row = lax.broadcasted_iota(jnp.int32, (nz, nr), 0)
@@ -161,66 +132,92 @@
     @pl.when(sec == 1)
     def _():
         def purge_body(t, carry):
-            base = t * (beds * beds)
+            srcs = [lax.rem(b + plan[t, b], beds) for b in range(beds)]
+            opens = [jnp.full((1, nr), valve[t, b], jnp.int32) != 0 for b in range(beds)]
             for c in range(3):
                 ys = [st[t, c, b, nz - 1 : nz, :] for b in range(beds)]
                 ls = [ad[t, c, b, nz - 1 : nz, :] for b in range(beds)]
                 for b in range(beds):
-                    gain = tbl[beds * beds * inst + t * beds + b]
-                    inc = tbl[base + b * beds] * ys[0]
-                    for bp in range(1, beds):
-                        inc = inc + tbl[base + b * beds + bp] * ys[bp]
-                    res[t, c, b, nz - 1 : nz, :] = res[t, c, b, nz - 1 : nz, :] + gain * (ys[b] - inc)
-                    back = gain * ls[b]
+                    inc = jnp.zeros((1, nr), jnp.float32)
+                    for bp in range(beds):
+                        inc = inc + jnp.where(srcs[b] == bp, ys[bp], 0.0)
+                    term = jnp.where(opens[b], PURGE_GAIN * (ys[b] - inc), 0.0)
+                    res[t, c, b, nz - 1 : nz, :] = res[t, c, b, nz - 1 : nz, :] + term
+                    back = jnp.where(opens[b], PURGE_GAIN * ls[b], 0.0)
                     for bb in range(beds):
-                        w = tbl[base + bb * beds + b] * tbl[beds * beds * inst + t * beds + bb]
-                        back = back - w * ls[bb]
+                        hit = jnp.logical_and(opens[bb], srcs[bb] == b)
+                        back = back - jnp.where(hit, PURGE_GAIN * ls[bb], 0.0)
                     adj[t, c, b, nz - 1 : nz, :] = adj[t, c, b, nz - 1 : nz, :] + back
             return carry
 
         lax.fori_loop(0, inst, purge_body, 0)
 
-    leg_st.wait_recv()
-    on_st = rcopy(ry_st, rv_st.at[1 - core], 6, fwd_st)
-    leg_ad.wait_recv()
-    on_ad = rcopy(ry_ad, rv_ad.at[1 - core], 7, fwd_ad)
-    for cp in (near_st, near_ad, on_st, on_ad):
-        cp.wait_recv()
-
-    def pick(own, recvd, j, c):
-        if j < 0:
-            return recvd[0, j + inst, c]
-        if j >= inst:
-            return recvd[1, j - inst, c]
-        return own[j, c]
-
-    def time_body(c, carry):
-        for t in range(inst):
-            acc_s = None
-            acc_a = None
-            for k, w in enumerate(STENCIL):
-                s = k + 1
-                ds = w * (pick(st, rv_st, t + s, c) - pick(st, rv_st, t - s, c))
-                da = w * (pick(ad, rv_ad, t + s, c) - pick(ad, rv_ad, t - s, c))
-                acc_s = ds if acc_s is None else acc_s + ds
-                acc_a = da if acc_a is None else acc_a + da
-            res[t, c] = TIME_SCALE * acc_s + res[t, c]
-            adj[t, c] = adj[t, c] - TIME_SCALE * acc_a
-        return carry
-
-    lax.fori_loop(0, comp, time_body, 0)
-    for cp in (leg_st, leg_ad, near_st, near_ad, on_st, on_ad):
+    def time_pass(cross_right, use_far):
+        def body(c, carry):
+            for t in range(inst):
+                acc_s = None
+                acc_a = None
+                for k, w in enumerate(STENCIL):
+                    s = k + 1
+                    d_s = None
+                    d_a = None
+                    for j, sign in ((t + s, 1.0), (t - s, -1.0)):
+                        if j >= inst:
+                            far = cross_right
+                            xs, xa = rv_st[1, j - inst, c], rv_ad[1, j - inst, c]
+                        elif j < 0:
+                            far = not cross_right
+                            xs, xa = rv_st[0, j + inst, c], rv_ad[0, j + inst, c]
+                        else:
+                            far = False
+                            xs, xa = st[j, c], ad[j, c]
+                        if far != use_far:
+                            continue
+                        if sign < 0:
+                            xs, xa = -xs, -xa
+                        d_s = xs if d_s is None else d_s + xs
+                        d_a = xa if d_a is None else d_a + xa
+                    if d_s is None:
+                        continue
+                    acc_s = w * d_s if acc_s is None else acc_s + w * d_s
+                    acc_a = w * d_a if acc_a is None else acc_a + w * d_a
+                if acc_s is None:
+                    continue
+                res[t, c] = TIME_SCALE * acc_s + res[t, c]
+                adj[t, c] = adj[t, c] - TIME_SCALE * acc_a
+            return carry
+
+        lax.fori_loop(0, comp, body, 0)
+
+    near_st.wait_recv()
+    near_ad.wait_recv()
+
+    @pl.when(core == 0)
+    def _():
+        time_pass(False, False)
+
+    @pl.when(core == 1)
+    def _():
+        time_pass(True, False)
+
+    far_st.wait_recv()
+    far_ad.wait_recv()
+
+    @pl.when(core == 0)
+    def _():
+        time_pass(False, True)
+
+    @pl.when(core == 1)
+    def _():
+        time_pass(True, True)
+
+    for cp in halo_copies + [far_st, far_ad, near_st, near_ad]:
         cp.wait_send()
 
 
 def local(state, adjoint, plan, valve):
     n_tm = lax.axis_size("tm")
     inst, comp, beds, nz, nr = state.shape
-    bed_ids = jnp.arange(beds, dtype=jnp.int32)
-    source = (bed_ids[None, :] + plan) % beds
-    onehot = (source[:, :, None] == bed_ids[None, None, :]).astype(jnp.float32)
-    gain = PURGE_GAIN * valve.astype(jnp.float32)
-    tbl = jnp.concatenate([onehot.reshape(-1), gain.reshape(-1)])
     block = jax.ShapeDtypeStruct(state.shape, jnp.float32)
     vmem = pl.BlockSpec(memory_space=pltpu.VMEM)
     halo_shape = (inst, comp, beds, 8, nr)
@@ -231,14 +228,13 @@
     res, adj = pl.pallas_call(
         kern,
         out_shape=(block, block),
-        in_specs=[pl.BlockSpec(memory_space=pltpu.SMEM), vmem, vmem],
+        in_specs=[pl.BlockSpec(memory_space=pltpu.SMEM)] * 2 + [vmem, vmem],
         out_specs=(vmem, vmem),
         scratch_shapes=[pltpu.VMEM((2,) + state.shape, jnp.float32)] * 2
-        + [pltpu.VMEM(state.shape, jnp.float32)] * 2
         + [pltpu.VMEM(halo_shape, jnp.float32)] * 2
-        + [pltpu.SemaphoreType.DMA((8,)), pltpu.SemaphoreType.DMA((8,))],
+        + [pltpu.SemaphoreType.DMA((6,)), pltpu.SemaphoreType.DMA((6,))],
         compiler_params=pltpu.CompilerParams(collective_id=0, has_side_effects=True),
-    )(tbl, state, adjoint)
+    )(plan, valve, state, adjoint)
     return res, adj
 
 

time: 60.7 us -> 49.1 us (0.81)
  Pallas kernels: 55.2 us -> 45.2 us
  other arithmetic: 1.36 us -> 0 us
    pallas_call x1, Pallas kernels: 55.2 us -> 45.2 us  [local(): pl.pallas_call(kern, out_shape=(block, block), in_specs=[pl.BlockSpec(mem...]
    select_n x1 -> x0, other arithmetic: 0.7 us -> none  [local(): source = (bed_ids[None, :] + plan) % beds]
    unnamed x6 -> x4, local copies, waits for them, and re-layouts: 3.05 us -> 3.04 us
where the time goes in v3:
time: 49.1 us; the launch traced here: 48.9 us
  Pallas kernels  45.2 us (92%)
  local copies, waits for them, and re-layouts  3.04 us (6%)
  between operations  0.65 us (1%)
    pallas_call x1, Pallas kernels, local(): pl.pallas_call(kern, out_shape=(block, block), in_specs=[pl.BlockSpec(mem...  45.2 us
    unnamed x4, local copies, waits for them, and re-layouts  3.04 us

profile of v3, /device:TPU:1, one launch (start us, length us, event | category | flops | bytes accessed | tf_op | source)
XLA Modules:
  0.0 48.9 jit_solution(12022807526362794548)
XLA Ops:
  0.6 45.2 %shard_map.59 = (f32[4,6,4,16,128]{4,3,2,1,0:T(8,128)}, f32[4,6,4,16,128]{4,3,2,1,0:T(8,128)}) custom-call(s32[4,4]{1,0:T(4,128)} %refs_0_.1, s32[4,4]{1,0:T(4,128)} %refs_1_.1, f32[4,6,4,16,128]{4,3,2,1,0:T(8,128)} %refs_2_.1, f32[4,6,4,16,128]{4,3,2,1,0:T(8,128)} %refs_3_.1), custom_call_target="tpu_custom_call" | custom-call | tf_op jit(solution)/shard_map/pallas_call | solution.py:228
  45.9 0.0 copy-start
  45.9 2.2 %copy.8 = f32[4,6,4,16,128]{4,3,2,1,0:T(8,128)} copy(f32[4,6,4,16,128]{4,3,2,1,0:T(8,128)} %get-tuple-element.4) | data formatting | bytes 1572864
  48.0 0.0 copy-done
  48.0 0.9 %copy.9 = f32[4,6,4,16,128]{4,3,2,1,0:T(8,128)} copy(f32[4,6,4,16,128]{4,3,2,1,0:T(8,128)S(1)} %copy-done) | data formatting | bytes 1572864
Async XLA Ops:
  45.9 2.2 %copy-start = (f32[4,6,4,16,128]{4,3,2,1,0:T(8,128)S(1)}, f32[4,6,4,16,128]{4,3,2,1,0:T(8,128)}, u32[]{:S(2)}) copy-start(f32[4,6,4,16,128]{4,3,2,1,0:T(8,128)} %get-tuple-element.5) | copy-start | bytes 2359300

commit v4 on v3

--- a/solution.py
+++ b/solution.py
@@ -20,35 +20,91 @@
 MESH = pl.DeviceIdType.MESH
 
 
-def _kernel(n_tm, plan, valve, st, ad, res, adj, rv_st, rv_ad, h_st, h_ad, send, recv):
+def _kernel(n_tm, plan, valve, st, ad, res, adj, rv_st, rv_ad, h_st, h_ad, ry_st, ry_ad, send, recv):
     inst, comp, beds, nz, nr = st.shape
     me = lax.axis_index("tm")
     sec = lax.axis_index("sec")
     core = lax.rem(me, 2)
+    ring = lax.div(me, 4)
+    y = lax.rem(lax.div(me, 2), 2) * 2 + sec
     pair = (me + 1 - 2 * core, sec)
     cross = (lax.rem(me + 2 * core - 1 + n_tm, n_tm), sec)
     partner = (me, 1 - sec)
 
+    def at(yy, cc):
+        yy = lax.rem(yy, 4)
+        return (ring * 4 + lax.div(yy, 2) * 2 + cc, lax.rem(yy, 2))
+
+    is_pure = (core + lax.div(y, 2)) == 1
+    is_relay = (core + lax.div(lax.rem(y + 1, 4), 2)) == 1
+    relay_of_me = at(y + 3, core)
+    relay_to_me = at(y + 1, 1 - core)
+    source = at(y + 1, core)
+    dest = at(y + 3, 1 - core)
+
     barrier = pltpu.get_barrier_semaphore()
     for dev in (pair, cross, partner):
         pl.semaphore_signal(barrier, inc=1, device_id=dev, device_id_type=MESH)
-    pl.semaphore_wait(barrier, 3)
-
-    def rcopy(src, dst, i, dev):
-        cp = pltpu.make_async_remote_copy(
+
+    @pl.when(is_pure)
+    def _():
+        for dev in (relay_of_me, relay_to_me):
+            pl.semaphore_signal(barrier, inc=1, device_id=dev, device_id_type=MESH)
+
+    @pl.when(is_relay)
+    def _():
+        for dev in (source, dest):
+            pl.semaphore_signal(barrier, inc=1, device_id=dev, device_id_type=MESH)
+
+    pl.semaphore_wait(barrier, 3 + 2 * is_pure.astype(jnp.int32) + 2 * is_relay.astype(jnp.int32))
+
+    def desc(src, dst, i, dev):
+        return pltpu.make_async_remote_copy(
             src_ref=src, dst_ref=dst, send_sem=send.at[i], recv_sem=recv.at[i],
             device_id=dev, device_id_type=MESH,
         )
+
+    def rcopy(src, dst, i, dev):
+        cp = desc(src, dst, i, dev)
         cp.start()
         return cp
+
+    split = inst - 1
+
+    def far_descs(n):
+        return [
+            desc(st.at[0:n], rv_st.at[1 - core, 0:n], 0, cross),
+            desc(ad.at[0:n], rv_ad.at[1 - core, 0:n], 1, cross),
+        ]
+
+    def leg_descs():
+        return [
+            desc(st.at[split:inst], ry_st, 6, relay_of_me),
+            desc(ad.at[split:inst], ry_ad, 7, relay_of_me),
+        ]
+
+    def fwd_descs():
+        return [
+            desc(ry_st, rv_st.at[1 - core, split:inst], 8, dest),
+            desc(ry_ad, rv_ad.at[1 - core, split:inst], 9, dest),
+        ]
 
     row_src = (nz - 1) * (1 - sec)
     halo_copies = [
         rcopy(src.at[:, :, :, pl.ds(row_src, 1), :], dst.at[:, :, :, pl.ds(0, 1), :], 4 + i, partner)
         for i, (src, dst) in enumerate(((st, h_st), (ad, h_ad)))
     ]
-    far_st = rcopy(st, rv_st.at[1 - core], 0, cross)
-    far_ad = rcopy(ad, rv_ad.at[1 - core], 1, cross)
+
+    @pl.when(is_pure)
+    def _():
+        for cp in far_descs(split) + leg_descs():
+            cp.start()
+
+    @pl.when(jnp.logical_not(is_pure))
+    def _():
+        for cp in far_descs(inst):
+            cp.start()
+
     near_st = rcopy(st, rv_st.at[core], 2, pair)
     near_ad = rcopy(ad, rv_ad.at[core], 3, pair)
 
@@ -189,6 +245,12 @@
 
         lax.fori_loop(0, comp, body, 0)
 
+    @pl.when(is_relay)
+    def _():
+        for leg, fwd in zip(leg_descs(), fwd_descs()):
+            leg.wait_recv()
+            fwd.start()
+
     near_st.wait_recv()
     near_ad.wait_recv()
 
@@ -200,8 +262,15 @@
     def _():
         time_pass(True, False)
 
-    far_st.wait_recv()
-    far_ad.wait_recv()
+    @pl.when(is_pure)
+    def _():
+        for cp in far_descs(split) + fwd_descs():
+            cp.wait_recv()
+
+    @pl.when(jnp.logical_not(is_pure))
+    def _():
+        for cp in far_descs(inst):
+            cp.wait_recv()
 
     @pl.when(core == 0)
     def _():
@@ -211,8 +280,23 @@
     def _():
         time_pass(True, True)
 
-    for cp in halo_copies + [far_st, far_ad, near_st, near_ad]:
+    for cp in halo_copies + [near_st, near_ad]:
         cp.wait_send()
+
+    @pl.when(is_pure)
+    def _():
+        for cp in far_descs(split) + leg_descs():
+            cp.wait_send()
+
+    @pl.when(jnp.logical_not(is_pure))
+    def _():
+        for cp in far_descs(inst):
+            cp.wait_send()
+
+    @pl.when(is_relay)
+    def _():
+        for cp in fwd_descs():
+            cp.wait_send()
 
 
 def local(state, adjoint, plan, valve):
@@ -232,7 +316,8 @@
         out_specs=(vmem, vmem),
         scratch_shapes=[pltpu.VMEM((2,) + state.shape, jnp.float32)] * 2
         + [pltpu.VMEM(halo_shape, jnp.float32)] * 2
-        + [pltpu.SemaphoreType.DMA((6,)), pltpu.SemaphoreType.DMA((6,))],
+        + [pltpu.VMEM((1,) + state.shape[1:], jnp.float32)] * 2
+        + [pltpu.SemaphoreType.DMA((10,)), pltpu.SemaphoreType.DMA((10,))],
         compiler_params=pltpu.CompilerParams(collective_id=0, has_side_effects=True),
     )(plan, valve, state, adjoint)
     return res, adj

time: 49.1 us -> 56 us (1.14); the launches traced: 48.9 us -> 54.9 us
  Pallas kernels: 45.2 us -> 51.2 us
    pallas_call x1, Pallas kernels: 45.2 us -> 51.2 us  [local(): pl.pallas_call(kern, out_shape=(block, block), in_specs=[pl.BlockSpec(mem...]
where the time goes in v4:
time: 56 us; the launch traced here: 54.9 us
  Pallas kernels  51.2 us (91%)
  local copies, waits for them, and re-layouts  3.04 us (5%)
  between operations  0.65 us (1%)
    pallas_call x1, Pallas kernels, local(): pl.pallas_call(kern, out_shape=(block, block), in_specs=[pl.BlockSpec(mem...  51.2 us
    unnamed x4, local copies, waits for them, and re-layouts  3.04 us

profile of v4, /device:TPU:1, one launch (start us, length us, event | category | flops | bytes accessed | tf_op | source)
XLA Modules:
  0.0 54.9 jit_solution(8148780221068702325)
XLA Ops:
  0.6 51.2 %shard_map.59 = (f32[4,6,4,16,128]{4,3,2,1,0:T(8,128)}, f32[4,6,4,16,128]{4,3,2,1,0:T(8,128)}) custom-call(s32[4,4]{1,0:T(4,128)} %refs_0_.1, s32[4,4]{1,0:T(4,128)} %refs_1_.1, f32[4,6,4,16,128]{4,3,2,1,0:T(8,128)} %refs_2_.1, f32[4,6,4,16,128]{4,3,2,1,0:T(8,128)} %refs_3_.1), custom_call_target="tpu_custom_call" | custom-call | tf_op jit(solution)/shard_map/pallas_call | solution.py:312
  51.8 0.0 copy-start
  51.8 2.2 %copy.8 = f32[4,6,4,16,128]{4,3,2,1,0:T(8,128)} copy(f32[4,6,4,16,128]{4,3,2,1,0:T(8,128)} %get-tuple-element.4) | data formatting | bytes 1572864
  54.0 0.0 copy-done
  54.0 0.9 %copy.9 = f32[4,6,4,16,128]{4,3,2,1,0:T(8,128)} copy(f32[4,6,4,16,128]{4,3,2,1,0:T(8,128)S(1)} %copy-done) | data formatting | bytes 1572864
Async XLA Ops:
  51.8 2.2 %copy-start = (f32[4,6,4,16,128]{4,3,2,1,0:T(8,128)S(1)}, f32[4,6,4,16,128]{4,3,2,1,0:T(8,128)}, u32[]{:S(2)}) copy-start(f32[4,6,4,16,128]{4,3,2,1,0:T(8,128)} %get-tuple-element.5) | copy-start | bytes 2359300

commit v5 on v4

--- a/solution.py
+++ b/solution.py
@@ -36,11 +36,11 @@
         return (ring * 4 + lax.div(yy, 2) * 2 + cc, lax.rem(yy, 2))
 
     is_pure = (core + lax.div(y, 2)) == 1
-    is_relay = (core + lax.div(lax.rem(y + 1, 4), 2)) == 1
-    relay_of_me = at(y + 3, core)
-    relay_to_me = at(y + 1, 1 - core)
-    source = at(y + 1, core)
-    dest = at(y + 3, 1 - core)
+    is_relay = (core + lax.div(lax.rem(y + 3, 4), 2)) == 1
+    relay_of_me = at(y + 1, core)
+    relay_to_me = at(y + 3, 1 - core)
+    source = at(y + 3, core)
+    dest = at(y + 1, 1 - core)
 
     barrier = pltpu.get_barrier_semaphore()
     for dev in (pair, cross, partner):

time: 56 us -> 57.7 us (1.030); the launches traced: 54.9 us -> 57.5 us
  Pallas kernels: 51.2 us -> 53.9 us
    pallas_call x1, Pallas kernels: 51.2 us -> 53.9 us  [local(): pl.pallas_call(kern, out_shape=(block, block), in_specs=[pl.BlockSpec(mem...]
where the time goes in v5:
time: 57.7 us; the launch traced here: 57.5 us
  Pallas kernels  53.9 us (93%)
  local copies, waits for them, and re-layouts  3.04 us (5%)
  between operations  0.65 us (1%)
    pallas_call x1, Pallas kernels, local(): pl.pallas_call(kern, out_shape=(block, block), in_specs=[pl.BlockSpec(mem...  53.9 us
    unnamed x4, local copies, waits for them, and re-layouts  3.04 us

profile of v5, /device:TPU:1, one launch (start us, length us, event | category | flops | bytes accessed | tf_op | source)
XLA Modules:
  0.0 57.5 jit_solution(8421364313854752452)
XLA Ops:
  0.6 53.9 %shard_map.59 = (f32[4,6,4,16,128]{4,3,2,1,0:T(8,128)}, f32[4,6,4,16,128]{4,3,2,1,0:T(8,128)}) custom-call(s32[4,4]{1,0:T(4,128)} %refs_0_.1, s32[4,4]{1,0:T(4,128)} %refs_1_.1, f32[4,6,4,16,128]{4,3,2,1,0:T(8,128)} %refs_2_.1, f32[4,6,4,16,128]{4,3,2,1,0:T(8,128)} %refs_3_.1), custom_call_target="tpu_custom_call" | custom-call | tf_op jit(solution)/shard_map/pallas_call | solution.py:312
  54.5 0.0 copy-start
  54.5 2.2 %copy.8 = f32[4,6,4,16,128]{4,3,2,1,0:T(8,128)} copy(f32[4,6,4,16,128]{4,3,2,1,0:T(8,128)} %get-tuple-element.4) | data formatting | bytes 1572864
  56.7 0.0 copy-done
  56.7 0.9 %copy.9 = f32[4,6,4,16,128]{4,3,2,1,0:T(8,128)} copy(f32[4,6,4,16,128]{4,3,2,1,0:T(8,128)S(1)} %copy-done) | data formatting | bytes 1572864
Async XLA Ops:
  54.5 2.2 %copy-start = (f32[4,6,4,16,128]{4,3,2,1,0:T(8,128)S(1)}, f32[4,6,4,16,128]{4,3,2,1,0:T(8,128)}, u32[]{:S(2)}) copy-start(f32[4,6,4,16,128]{4,3,2,1,0:T(8,128)} %get-tuple-element.5) | copy-start | bytes 2359300

commit v6 on v3

--- a/solution.py
+++ b/solution.py
@@ -47,8 +47,19 @@
         rcopy(src.at[:, :, :, pl.ds(row_src, 1), :], dst.at[:, :, :, pl.ds(0, 1), :], 4 + i, partner)
         for i, (src, dst) in enumerate(((st, h_st), (ad, h_ad)))
     ]
-    far_st = rcopy(st, rv_st.at[1 - core], 0, cross)
-    far_ad = rcopy(ad, rv_ad.at[1 - core], 1, cross)
+    def desc(src, dst, i, dev):
+        return pltpu.make_async_remote_copy(
+            src_ref=src, dst_ref=dst, send_sem=send.at[i], recv_sem=recv.at[i],
+            device_id=dev, device_id_type=MESH,
+        )
+
+    def chunked(src, dst, i, dev):
+        for j in range(inst):
+            desc(src.at[j : j + 1], dst.at[j : j + 1], i, dev).start()
+        return desc(src, dst, i, dev)
+
+    far_st = chunked(st, rv_st.at[1 - core], 0, cross)
+    far_ad = chunked(ad, rv_ad.at[1 - core], 1, cross)
     near_st = rcopy(st, rv_st.at[core], 2, pair)
     near_ad = rcopy(ad, rv_ad.at[core], 3, pair)
 

time: 49.1 us -> 49.1 us (level)
  no operation moved by 1% of the time
where the time goes in v6:
time: 49.1 us; the launch traced here: 48.9 us
  Pallas kernels  45.2 us (92%)
  local copies, waits for them, and re-layouts  3.04 us (6%)
  between operations  0.65 us (1%)
    pallas_call x1, Pallas kernels, local(): pl.pallas_call(kern, out_shape=(block, block), in_specs=[pl.BlockSpec(mem...  45.2 us
    unnamed x4, local copies, waits for them, and re-layouts  3.04 us

profile of v6, /device:TPU:1, one launch (start us, length us, event | category | flops | bytes accessed | tf_op | source)
XLA Modules:
  0.0 48.9 jit_solution(4641533745266748671)
XLA Ops:
  0.6 45.2 %shard_map.59 = (f32[4,6,4,16,128]{4,3,2,1,0:T(8,128)}, f32[4,6,4,16,128]{4,3,2,1,0:T(8,128)}) custom-call(s32[4,4]{1,0:T(4,128)} %refs_0_.1, s32[4,4]{1,0:T(4,128)} %refs_1_.1, f32[4,6,4,16,128]{4,3,2,1,0:T(8,128)} %refs_2_.1, f32[4,6,4,16,128]{4,3,2,1,0:T(8,128)} %refs_3_.1), custom_call_target="tpu_custom_call" | custom-call | tf_op jit(solution)/shard_map/pallas_call | solution.py:239
  45.9 0.0 copy-start
  45.9 2.2 %copy.8 = f32[4,6,4,16,128]{4,3,2,1,0:T(8,128)} copy(f32[4,6,4,16,128]{4,3,2,1,0:T(8,128)} %get-tuple-element.4) | data formatting | bytes 1572864
  48.0 0.0 copy-done
  48.0 0.9 %copy.9 = f32[4,6,4,16,128]{4,3,2,1,0:T(8,128)} copy(f32[4,6,4,16,128]{4,3,2,1,0:T(8,128)S(1)} %copy-done) | data formatting | bytes 1572864
Async XLA Ops:
  45.9 2.2 %copy-start = (f32[4,6,4,16,128]{4,3,2,1,0:T(8,128)S(1)}, f32[4,6,4,16,128]{4,3,2,1,0:T(8,128)}, u32[]{:S(2)}) copy-start(f32[4,6,4,16,128]{4,3,2,1,0:T(8,128)} %get-tuple-element.5) | copy-start | bytes 2359300

commit v7 on v3

--- a/solution.py
+++ b/solution.py
@@ -20,7 +20,7 @@
 MESH = pl.DeviceIdType.MESH
 
 
-def _kernel(n_tm, plan, valve, st, ad, res, adj, rv_st, rv_ad, h_st, h_ad, send, recv):
+def _kernel(n_tm, plan, valve, st, ad, res, adj, x_st, x_ad, n_st, n_ad, h_st, h_ad, send, recv):
     inst, comp, beds, nz, nr = st.shape
     me = lax.axis_index("tm")
     sec = lax.axis_index("sec")
@@ -47,10 +47,10 @@
         rcopy(src.at[:, :, :, pl.ds(row_src, 1), :], dst.at[:, :, :, pl.ds(0, 1), :], 4 + i, partner)
         for i, (src, dst) in enumerate(((st, h_st), (ad, h_ad)))
     ]
-    far_st = rcopy(st, rv_st.at[1 - core], 0, cross)
-    far_ad = rcopy(ad, rv_ad.at[1 - core], 1, cross)
-    near_st = rcopy(st, rv_st.at[core], 2, pair)
-    near_ad = rcopy(ad, rv_ad.at[core], 3, pair)
+    far_st = rcopy(st, x_st, 0, cross)
+    far_ad = rcopy(ad, x_ad, 1, cross)
+    near_st = rcopy(st, n_st, 2, pair)
+    near_ad = rcopy(ad, n_ad, 3, pair)
 
     for cp in halo_copies:
         cp.wait_recv()
@@ -152,67 +152,78 @@
 
         lax.fori_loop(0, inst, purge_body, 0)
 
-    def time_pass(cross_right, use_far):
-        def body(c, carry):
-            for t in range(inst):
-                acc_s = None
-                acc_a = None
-                for k, w in enumerate(STENCIL):
-                    s = k + 1
-                    d_s = None
-                    d_a = None
-                    for j, sign in ((t + s, 1.0), (t - s, -1.0)):
-                        if j >= inst:
-                            far = cross_right
-                            xs, xa = rv_st[1, j - inst, c], rv_ad[1, j - inst, c]
-                        elif j < 0:
-                            far = not cross_right
-                            xs, xa = rv_st[0, j + inst, c], rv_ad[0, j + inst, c]
-                        else:
-                            far = False
-                            xs, xa = st[j, c], ad[j, c]
-                        if far != use_far:
-                            continue
-                        if sign < 0:
-                            xs, xa = -xs, -xa
-                        d_s = xs if d_s is None else d_s + xs
-                        d_a = xa if d_a is None else d_a + xa
-                    if d_s is None:
-                        continue
-                    acc_s = w * d_s if acc_s is None else acc_s + w * d_s
-                    acc_a = w * d_a if acc_a is None else acc_a + w * d_a
-                if acc_s is None:
-                    continue
-                res[t, c] = TIME_SCALE * acc_s + res[t, c]
-                adj[t, c] = adj[t, c] - TIME_SCALE * acc_a
-            return carry
-
-        lax.fori_loop(0, comp, body, 0)
-
     near_st.wait_recv()
     near_ad.wait_recv()
 
     @pl.when(core == 0)
     def _():
-        time_pass(False, False)
+        _time_terms(res, adj, res, adj, st, ad, None, (n_st, n_ad), False, False)
 
     @pl.when(core == 1)
     def _():
-        time_pass(True, False)
+        _time_terms(res, adj, res, adj, st, ad, (n_st, n_ad), None, True, False)
 
     far_st.wait_recv()
     far_ad.wait_recv()
 
-    @pl.when(core == 0)
-    def _():
-        time_pass(False, True)
-
-    @pl.when(core == 1)
-    def _():
-        time_pass(True, True)
-
     for cp in halo_copies + [far_st, far_ad, near_st, near_ad]:
         cp.wait_send()
+
+
+def _time_terms(out_res, out_adj, in_res, in_adj, st, ad, lo, hi, cross_right, use_far):
+    inst, comp = st.shape[0], st.shape[1]
+
+    def body(c, carry):
+        for t in range(inst):
+            acc_s = None
+            acc_a = None
+            for k, w in enumerate(STENCIL):
+                s = k + 1
+                d_s = None
+                d_a = None
+                for j, sign in ((t + s, 1.0), (t - s, -1.0)):
+                    if j >= inst:
+                        far = cross_right
+                    elif j < 0:
+                        far = not cross_right
+                    else:
+                        far = False
+                    if far != use_far:
+                        continue
+                    if j >= inst:
+                        pair = (hi[0], hi[1], j - inst)
+                    elif j < 0:
+                        pair = (lo[0], lo[1], j + inst)
+                    else:
+                        pair = (st, ad, j)
+                    xs, xa = pair[0][pair[2], c], pair[1][pair[2], c]
+                    if sign < 0:
+                        xs, xa = -xs, -xa
+                    d_s = xs if d_s is None else d_s + xs
+                    d_a = xa if d_a is None else d_a + xa
+                if d_s is None:
+                    continue
+                acc_s = w * d_s if acc_s is None else acc_s + w * d_s
+                acc_a = w * d_a if acc_a is None else acc_a + w * d_a
+            if acc_s is None:
+                continue
+            out_res[t, c] = TIME_SCALE * acc_s + in_res[t, c]
+            out_adj[t, c] = in_adj[t, c] - TIME_SCALE * acc_a
+        return carry
+
+    lax.fori_loop(0, comp, body, 0)
+
+
+def _finish(x_st, x_ad, res_p, adj_p, res, adj):
+    core = lax.rem(lax.axis_index("tm"), 2)
+
+    @pl.when(core == 0)
+    def _():
+        _time_terms(res, adj, res_p, adj_p, x_st, x_ad, (x_st, x_ad), None, False, True)
+
+    @pl.when(core == 1)
+    def _():
+        _time_terms(res, adj, res_p, adj_p, x_st, x_ad, None, (x_st, x_ad), True, True)
 
 
 def local(state, adjoint, plan, valve):
@@ -225,16 +236,22 @@
     def kern(*refs):
         _kernel(n_tm, *refs)
 
-    res, adj = pl.pallas_call(
+    res_p, adj_p, x_st, x_ad = pl.pallas_call(
         kern,
-        out_shape=(block, block),
+        out_shape=(block,) * 4,
         in_specs=[pl.BlockSpec(memory_space=pltpu.SMEM)] * 2 + [vmem, vmem],
-        out_specs=(vmem, vmem),
-        scratch_shapes=[pltpu.VMEM((2,) + state.shape, jnp.float32)] * 2
+        out_specs=(vmem,) * 4,
+        scratch_shapes=[pltpu.VMEM(state.shape, jnp.float32)] * 2
         + [pltpu.VMEM(halo_shape, jnp.float32)] * 2
         + [pltpu.SemaphoreType.DMA((6,)), pltpu.SemaphoreType.DMA((6,))],
         compiler_params=pltpu.CompilerParams(collective_id=0, has_side_effects=True),
     )(plan, valve, state, adjoint)
+    res, adj = pl.pallas_call(
+        _finish,
+        out_shape=(block, block),
+        in_specs=[vmem] * 4,
+        out_specs=(vmem, vmem),
+    )(x_st, x_ad, res_p, adj_p)
     return res, adj
 
 

time: 49.1 us -> 49.5 us (level)
  Pallas kernels: 45.2 us -> 48.7 us
  local copies, waits for them, and re-layouts: 3.04 us -> 0 us
    pallas_call x1 -> x2, Pallas kernels: 45.2 us -> 48.7 us  [the longest x1 45.3 us: local(): pl.pallas_call(kern, out_shape=(block,) * 4, in_specs=[pl.BlockSpec(memor...]
    unnamed x4 -> x0, local copies, waits for them, and re-layouts: 3.04 us -> none
where the time goes in v7:
time: 49.5 us; the launch traced here: 49.3 us
  Pallas kernels  48.7 us (98%)
  between operations  0.64 us (1%)
    pallas_call x1, Pallas kernels, local(): pl.pallas_call(kern, out_shape=(block,) * 4, in_specs=[pl.BlockSpec(memor...  45.3 us
    pallas_call x1, Pallas kernels, local(): pl.pallas_call(_finish, out_shape=(block, block), in_specs=[vmem] * 4, ou...  3.35 us

profile of v7, /device:TPU:1, one launch (start us, length us, event | category | flops | bytes accessed | tf_op | source)
XLA Modules:
  0.0 49.3 jit_solution(13951100645488101975)
XLA Ops:
  0.6 45.3 %shard_map.59 = (f32[4,6,4,16,128]{4,3,2,1,0:T(8,128)}, f32[4,6,4,16,128]{4,3,2,1,0:T(8,128)}, f32[4,6,4,16,128]{4,3,2,1,0:T(8,128)}, f32[4,6,4,16,128]{4,3,2,1,0:T(8,128)}) custom-call(s32[4,4]{1,0:T(4,128)} %refs_0_.1, s32[4,4]{1,0:T(4,128)} %refs_1_.1, f32[4,6,4,16,128]{4,3,2,1,0:T(8,128)} %refs_2_.1, f32[4,6,4,16,128]{4,3,2,1,0:T(8,128)} %refs_3_.1), custom_call_target="tpu_custom_call" | custom-call | tf_op jit(solution)/shard_map/pallas_call | solution.py:239
  46.0 3.3 %shard_map.60 = (f32[4,6,4,16,128]{4,3,2,1,0:T(8,128)}, f32[4,6,4,16,128]{4,3,2,1,0:T(8,128)}) custom-call(f32[4,6,4,16,128]{4,3,2,1,0:T(8,128)} %get-tuple-element.6.x_st, f32[4,6,4,16,128]{4,3,2,1,0:T(8,128)} %get-tuple-element.7.x_ad, f32[4,6,4,16,128]{4,3,2,1,0:T(8,128)} %get-tuple-element.8.res_p, f32[4,6,4,16,128]{4,3,2,1,0:T(8,128)} %get-tuple-element.9.adj_p), custom_call_target="tpu_custom_call" | custom-call | tf_op jit(solution)/shard_map/pallas_call | solution.py:249

commit v8 on v7

--- a/solution.py
+++ b/solution.py
@@ -246,11 +246,13 @@
         + [pltpu.SemaphoreType.DMA((6,)), pltpu.SemaphoreType.DMA((6,))],
         compiler_params=pltpu.CompilerParams(collective_id=0, has_side_effects=True),
     )(plan, valve, state, adjoint)
+    per_comp = pl.BlockSpec((inst, 1, beds, nz, nr), lambda c: (0, c, 0, 0, 0))
     res, adj = pl.pallas_call(
         _finish,
         out_shape=(block, block),
-        in_specs=[vmem] * 4,
-        out_specs=(vmem, vmem),
+        grid=(comp,),
+        in_specs=[per_comp] * 4,
+        out_specs=(per_comp, per_comp),
     )(x_st, x_ad, res_p, adj_p)
     return res, adj
 

time: 49.5 us -> 51.2 us (1.034)
  Pallas kernels: 48.7 us -> 50.4 us
    pallas_call x1, Pallas kernels: 3.35 us -> 5.03 us  [local(): pl.pallas_call(_finish, out_shape=(block, block), grid=(comp,), in_specs=...]
where the time goes in v8:
time: 51.2 us; the launch traced here: 51 us
  Pallas kernels  50.4 us (98%)
  between operations  0.64 us (1%)
    pallas_call x1, Pallas kernels, local(): pl.pallas_call(kern, out_shape=(block,) * 4, in_specs=[pl.BlockSpec(memor...  45.3 us
    pallas_call x1, Pallas kernels, local(): pl.pallas_call(_finish, out_shape=(block, block), grid=(comp,), in_specs=...  5.03 us

profile of v8, /device:TPU:1, one launch (start us, length us, event | category | flops | bytes accessed | tf_op | source)
XLA Modules:
  0.0 51.0 jit_solution(6426396325203490842)
XLA Ops:
  0.6 45.3 %shard_map.59 = (f32[4,6,4,16,128]{4,3,2,1,0:T(8,128)}, f32[4,6,4,16,128]{4,3,2,1,0:T(8,128)}, f32[4,6,4,16,128]{4,3,2,1,0:T(8,128)}, f32[4,6,4,16,128]{4,3,2,1,0:T(8,128)}) custom-call(s32[4,4]{1,0:T(4,128)} %refs_0_.1, s32[4,4]{1,0:T(4,128)} %refs_1_.1, f32[4,6,4,16,128]{4,3,2,1,0:T(8,128)} %refs_2_.1, f32[4,6,4,16,128]{4,3,2,1,0:T(8,128)} %refs_3_.1), custom_call_target="tpu_custom_call" | custom-call | tf_op jit(solution)/shard_map/pallas_call | solution.py:239
  46.0 5.0 %shard_map.60 = (f32[4,6,4,16,128]{4,3,2,1,0:T(8,128)}, f32[4,6,4,16,128]{4,3,2,1,0:T(8,128)}) custom-call(f32[4,6,4,16,128]{4,3,2,1,0:T(8,128)} %get-tuple-element.6.x_st, f32[4,6,4,16,128]{4,3,2,1,0:T(8,128)} %get-tuple-element.7.x_ad, f32[4,6,4,16,128]{4,3,2,1,0:T(8,128)} %get-tuple-element.8.res_p, f32[4,6,4,16,128]{4,3,2,1,0:T(8,128)} %get-tuple-element.9.adj_p), custom_call_target="tpu_custom_call" | custom-call | tf_op jit(solution)/shard_map/pallas_call | solution.py:250

commit v9 on v7

--- a/solution.py
+++ b/solution.py
@@ -246,12 +246,26 @@
         + [pltpu.SemaphoreType.DMA((6,)), pltpu.SemaphoreType.DMA((6,))],
         compiler_params=pltpu.CompilerParams(collective_id=0, has_side_effects=True),
     )(plan, valve, state, adjoint)
-    res, adj = pl.pallas_call(
-        _finish,
-        out_shape=(block, block),
-        in_specs=[vmem] * 4,
-        out_specs=(vmem, vmem),
-    )(x_st, x_ad, res_p, adj_p)
+    core = lax.rem(lax.axis_index("tm"), 2)
+
+    def cross_terms(x):
+        rows = []
+        for t in range(inst):
+            left = None
+            right = None
+            for k, w in enumerate(STENCIL):
+                s = k + 1
+                if t - s < 0:
+                    term = -w * x[t - s + inst]
+                    left = term if left is None else left + term
+                if t + s >= inst:
+                    term = w * x[t + s - inst]
+                    right = term if right is None else right + term
+            rows.append(jnp.where(core == 0, left, right))
+        return TIME_SCALE * jnp.stack(rows)
+
+    res = res_p + cross_terms(x_st)
+    adj = adj_p - cross_terms(x_ad)
     return res, adj
 
 

time: 49.5 us -> 50.5 us (1.020)
  Pallas kernels: 48.7 us -> 45.3 us
  other arithmetic: 0 us -> 3.21 us
  local copies, waits for them, and re-layouts: 0 us -> 1.1 us
    pallas_call x1 -> x0, Pallas kernels: 3.35 us -> none  [local(): pl.pallas_call(_finish, out_shape=(block, block), in_specs=[vmem] * 4, ou...]
    select_n x0 -> x2, other arithmetic: none -> 1.78 us  [cross_terms(): rows.append(jnp.where(core == 0, left, right))]
    add x0 -> x1, other arithmetic: none -> 1.43 us  [local(): res = res_p + cross_terms(x_st)]
    unnamed x0 -> x6, local copies, waits for them, and re-layouts: none -> 1.1 us
where the time goes in v9:
time: 50.5 us; the launch traced here: 50.3 us
  Pallas kernels  45.3 us (90%)
  other arithmetic  3.21 us (6%)
  local copies, waits for them, and re-layouts  1.1 us (2%)
  between operations  0.69 us (1%)
    pallas_call x1, Pallas kernels, local(): pl.pallas_call(kern, out_shape=(block,) * 4, in_specs=[pl.BlockSpec(memor...  45.3 us
    select_n x2, other arithmetic, cross_terms(): rows.append(jnp.where(core == 0, left, right))  1.78 us
    add x1, other arithmetic, local(): res = res_p + cross_terms(x_st)  1.43 us
    unnamed x6, local copies, waits for them, and re-layouts  1.1 us

profile of v9, /device:TPU:1, one launch (start us, length us, event | category | flops | bytes accessed | tf_op | source)
XLA Modules:
  0.0 50.3 jit_solution(14057335323865380413)
XLA Ops:
  0.6 45.3 %shard_map.59 = (f32[4,6,4,16,128]{4,3,2,1,0:T(8,128)}, f32[4,6,4,16,128]{4,3,2,1,0:T(8,128)}, f32[4,6,4,16,128]{4,3,2,1,0:T(8,128)}, f32[4,6,4,16,128]{4,3,2,1,0:T(8,128)}) custom-call(s32[4,4]{1,0:T(4,128)} %refs_0_.1, s32[4,4]{1,0:T(4,128)} %refs_1_.1, f32[4,6,4,16,128]{4,3,2,1,0:T(8,128)} %refs_2_.1, f32[4,6,4,16,128]{4,3,2,1,0:T(8,128)} %refs_3_.1), custom_call_target="tpu_custom_call" | custom-call | tf_op jit(solution)/shard_map/pallas_call | solution.py:239
  46.0 0.0 copy-start.2
  46.0 1.5 %multiply_select_fusion.1 = (f32[1,6,4,16,128]{4,3,2,1,0:T(8,128)S(1)}, f32[1,6,4,16,128]{4,3,2,1,0:T(8,128)S(1)}, f32[1,6,4,16,128]{4,3,2,1,0:T(8,128)S(1)}, f32[1,6,4,16,128]{4,3,2,1,0:T(8,128)S(1)}) fusion(f32[4,6,4,16,128]{4,3,2,1,0:T(8,128)} %get-tuple-element.7, pred[]{:T(512)S(6)} %eq.2), kind=kLoop, calls=%fused_computation.11 | loop fusion | flops 1769472 | bytes 1572865 | tf_op jit(solution)/shard_map/jit(_where)/select_n | solution.py:264
  47.5 0.0 copy-done.2
  47.5 0.0 copy-start
  47.5 0.0 copy-start.1
  47.6 0.3 multiply_select_fusion
  47.8 0.9 %copy-done = f32[4,6,4,16,128]{4,3,2,1,0:T(8,128)S(1)} copy-done((f32[4,6,4,16,128]{4,3,2,1,0:T(8,128)S(1)}, f32[4,6,4,16,128]{4,3,2,1,0:T(8,128)}, u32[]{:S(2)}) %copy-start) | copy-done | bytes 786456
  48.7 0.2 copy-done.1
  48.9 1.4 %fusion = (f32[4,6,4,16,128]{4,3,2,1,0:T(8,128)}, f32[4,6,4,16,128]{4,3,2,1,0:T(8,128)}) fusion(f32[4,6,4,16,128]{4,3,2,1,0:T(8,128)S(1)} %copy-done, f32[1,6,4,16,128]{4,3,2,1,0:T(8,128)S(1)} %get-tuple-element.15, f32[1,6,4,16,128]{4,3,2,1,0:T(8,128)S(1)} %get-tuple-element.17, f32[1,6,4,16,128]{4,3,2,1,0:T(8,128)S(1)} %get-tuple-element.16, ...), kind=kLoop, calls=%fused_computation.1 | loop fusion | flops 1966080 | bytes 4718592 | tf_op jit(solution)/shard_map/add | solution.py:267
Async XLA Ops:
  46.0 1.5 %copy-start.2 = (f32[4,6,4,16,128]{4,3,2,1,0:T(8,128)S(1)}, f32[4,6,4,16,128]{4,3,2,1,0:T(8,128)}, u32[]{:S(2)}) copy-start(f32[4,6,4,16,128]{4,3,2,1,0:T(8,128)} %get-tuple-element.9) | copy-start | bytes 2359300
  47.5 1.1 %copy-start = (f32[4,6,4,16,128]{4,3,2,1,0:T(8,128)S(1)}, f32[4,6,4,16,128]{4,3,2,1,0:T(8,128)}, u32[]{:S(2)}) copy-start(f32[4,6,4,16,128]{4,3,2,1,0:T(8,128)} %get-tuple-element.6) | copy-start | bytes 2359300
  47.5 1.4 %copy-start.1 = (f32[4,6,4,16,128]{4,3,2,1,0:T(8,128)S(1)}, f32[4,6,4,16,128]{4,3,2,1,0:T(8,128)}, u32[]{:S(2)}) copy-start(f32[4,6,4,16,128]{4,3,2,1,0:T(8,128)} %get-tuple-element.8) | copy-start | bytes 2359300

commit v10 on v6

--- a/solution.py
+++ b/solution.py
@@ -20,7 +20,7 @@
 MESH = pl.DeviceIdType.MESH
 
 
-def _kernel(n_tm, plan, valve, st, ad, res, adj, rv_st, rv_ad, h_st, h_ad, send, recv):
+def _kernel(n_tm, plan, valve, st, ad, res_out, adj_out, res, adj, rv_st, rv_ad, h_st, h_ad, send, recv, osem):
     inst, comp, beds, nz, nr = st.shape
     me = lax.axis_index("tm")
     sec = lax.axis_index("sec")
@@ -53,13 +53,15 @@
             device_id=dev, device_id_type=MESH,
         )
 
-    def chunked(src, dst, i, dev):
-        for j in range(inst):
-            desc(src.at[j : j + 1], dst.at[j : j + 1], i, dev).start()
-        return desc(src, dst, i, dev)
-
-    far_st = chunked(st, rv_st.at[1 - core], 0, cross)
-    far_ad = chunked(ad, rv_ad.at[1 - core], 1, cross)
+    def far_descs(c):
+        return (
+            desc(st.at[:, c], rv_st.at[1 - core, :, c], 6 + c, cross),
+            desc(ad.at[:, c], rv_ad.at[1 - core, :, c], 6 + comp + c, cross),
+        )
+
+    for c in range(comp):
+        for cp in far_descs(c):
+            cp.start()
     near_st = rcopy(st, rv_st.at[core], 2, pair)
     near_ad = rcopy(ad, rv_ad.at[core], 3, pair)
 
@@ -163,7 +165,7 @@
 
         lax.fori_loop(0, inst, purge_body, 0)
 
-    def time_pass(cross_right, use_far):
+    def time_pass(cross_right, use_far, comp_index=None):
         def body(c, carry):
             for t in range(inst):
                 acc_s = None
@@ -198,7 +200,10 @@
                 adj[t, c] = adj[t, c] - TIME_SCALE * acc_a
             return carry
 
-        lax.fori_loop(0, comp, body, 0)
+        if comp_index is None:
+            lax.fori_loop(0, comp, body, 0)
+        else:
+            body(comp_index, 0)
 
     near_st.wait_recv()
     near_ad.wait_recv()
@@ -211,18 +216,39 @@
     def _():
         time_pass(True, False)
 
-    far_st.wait_recv()
-    far_ad.wait_recv()
-
-    @pl.when(core == 0)
-    def _():
-        time_pass(False, True)
-
-    @pl.when(core == 1)
-    def _():
-        time_pass(True, True)
-
-    for cp in halo_copies + [far_st, far_ad, near_st, near_ad]:
+    def out_descs(c):
+        return (
+            pltpu.make_async_copy(res.at[:, c], res_out.at[:, c], osem.at[c]),
+            pltpu.make_async_copy(adj.at[:, c], adj_out.at[:, c], osem.at[comp + c]),
+        )
+
+    def far_body(c, carry):
+        for cp in far_descs(c):
+            cp.wait_recv()
+
+        @pl.when(core == 0)
+        def _():
+            time_pass(False, True, c)
+
+        @pl.when(core == 1)
+        def _():
+            time_pass(True, True, c)
+
+        for cp in out_descs(c):
+            cp.start()
+        return carry
+
+    lax.fori_loop(0, comp, far_body, 0)
+
+    def drain(c, carry):
+        for cp in out_descs(c):
+            cp.wait()
+        for cp in far_descs(c):
+            cp.wait_send()
+        return carry
+
+    lax.fori_loop(0, comp, drain, 0)
+    for cp in halo_copies + [near_st, near_ad]:
         cp.wait_send()
 
 
@@ -240,10 +266,12 @@
         kern,
         out_shape=(block, block),
         in_specs=[pl.BlockSpec(memory_space=pltpu.SMEM)] * 2 + [vmem, vmem],
-        out_specs=(vmem, vmem),
-        scratch_shapes=[pltpu.VMEM((2,) + state.shape, jnp.float32)] * 2
+        out_specs=(pl.BlockSpec(memory_space=pl.ANY),) * 2,
+        scratch_shapes=[pltpu.VMEM(state.shape, jnp.float32)] * 2
+        + [pltpu.VMEM((2,) + state.shape, jnp.float32)] * 2
         + [pltpu.VMEM(halo_shape, jnp.float32)] * 2
-        + [pltpu.SemaphoreType.DMA((6,)), pltpu.SemaphoreType.DMA((6,))],
+        + [pltpu.SemaphoreType.DMA((6 + 2 * comp,)), pltpu.SemaphoreType.DMA((6 + 2 * comp,))]
+        + [pltpu.SemaphoreType.DMA((2 * comp,))],
         compiler_params=pltpu.CompilerParams(collective_id=0, has_side_effects=True),
     )(plan, valve, state, adjoint)
     return res, adj

time: 49.1 us -> 48.6 us (0.990)
  no operation moved by 1% of the time
where the time goes in v10:
time: 48.6 us; the launch traced here: 48.5 us
  Pallas kernels  44.8 us (92%)
  local copies, waits for them, and re-layouts  3.04 us (6%)
  between operations  0.65 us (1%)
    pallas_call x1, Pallas kernels, local(): pl.pallas_call(kern, out_shape=(block, block), in_specs=[pl.BlockSpec(mem...  44.8 us
    unnamed x4, local copies, waits for them, and re-layouts  3.04 us

profile of v10, /device:TPU:1, one launch (start us, length us, event | category | flops | bytes accessed | tf_op | source)
XLA Modules:
  0.0 48.5 jit_solution(8763992158741055885)
XLA Ops:
  0.6 44.8 %shard_map.59 = (f32[4,6,4,16,128]{4,3,2,1,0:T(8,128)}, f32[4,6,4,16,128]{4,3,2,1,0:T(8,128)}) custom-call(s32[4,4]{1,0:T(4,128)} %refs_0_.1, s32[4,4]{1,0:T(4,128)} %refs_1_.1, f32[4,6,4,16,128]{4,3,2,1,0:T(8,128)} %refs_2_.1, f32[4,6,4,16,128]{4,3,2,1,0:T(8,128)} %refs_3_.1), custom_call_target="tpu_custom_call" | custom-call | tf_op jit(solution)/shard_map/pallas_call | solution.py:265
  45.4 0.0 copy-start
  45.4 2.2 %copy.8 = f32[4,6,4,16,128]{4,3,2,1,0:T(8,128)} copy(f32[4,6,4,16,128]{4,3,2,1,0:T(8,128)} %get-tuple-element.4) | data formatting | bytes 1572864
  47.6 0.0 copy-done
  47.6 0.9 %copy.9 = f32[4,6,4,16,128]{4,3,2,1,0:T(8,128)} copy(f32[4,6,4,16,128]{4,3,2,1,0:T(8,128)S(1)} %copy-done) | data formatting | bytes 1572864
Async XLA Ops:
  45.4 2.2 %copy-start = (f32[4,6,4,16,128]{4,3,2,1,0:T(8,128)S(1)}, f32[4,6,4,16,128]{4,3,2,1,0:T(8,128)}, u32[]{:S(2)}) copy-start(f32[4,6,4,16,128]{4,3,2,1,0:T(8,128)} %get-tuple-element.5) | copy-start | bytes 2359300

commit v11 on v10

--- a/solution.py
+++ b/solution.py
@@ -20,7 +20,7 @@
 MESH = pl.DeviceIdType.MESH
 
 
-def _kernel(n_tm, plan, valve, st, ad, res_out, adj_out, res, adj, rv_st, rv_ad, h_st, h_ad, send, recv, osem):
+def _kernel(n_tm, plan, valve, st_hbm, ad_hbm, res_out, adj_out, st, ad, res, adj, rv_st, rv_ad, h_st, h_ad, send, recv, osem, lsem):
     inst, comp, beds, nz, nr = st.shape
     me = lax.axis_index("tm")
     sec = lax.axis_index("sec")
@@ -29,6 +29,13 @@
     cross = (lax.rem(me + 2 * core - 1 + n_tm, n_tm), sec)
     partner = (me, 1 - sec)
 
+    loads = [
+        pltpu.make_async_copy(st_hbm, st, lsem.at[0]),
+        pltpu.make_async_copy(ad_hbm, ad, lsem.at[1]),
+    ]
+    for cp in loads:
+        cp.start()
+
     barrier = pltpu.get_barrier_semaphore()
     for dev in (pair, cross, partner):
         pl.semaphore_signal(barrier, inc=1, device_id=dev, device_id_type=MESH)
@@ -45,7 +52,7 @@
     row_src = (nz - 1) * (1 - sec)
     halo_copies = [
         rcopy(src.at[:, :, :, pl.ds(row_src, 1), :], dst.at[:, :, :, pl.ds(0, 1), :], 4 + i, partner)
-        for i, (src, dst) in enumerate(((st, h_st), (ad, h_ad)))
+        for i, (src, dst) in enumerate(((st_hbm, h_st), (ad_hbm, h_ad)))
     ]
     def desc(src, dst, i, dev):
         return pltpu.make_async_remote_copy(
@@ -55,15 +62,17 @@
 
     def far_descs(c):
         return (
-            desc(st.at[:, c], rv_st.at[1 - core, :, c], 6 + c, cross),
-            desc(ad.at[:, c], rv_ad.at[1 - core, :, c], 6 + comp + c, cross),
+            desc(st_hbm.at[:, c], rv_st.at[1 - core, :, c], 6 + c, cross),
+            desc(ad_hbm.at[:, c], rv_ad.at[1 - core, :, c], 6 + comp + c, cross),
         )
 
     for c in range(comp):
         for cp in far_descs(c):
             cp.start()
-    near_st = rcopy(st, rv_st.at[core], 2, pair)
-    near_ad = rcopy(ad, rv_ad.at[core], 3, pair)
+    near_st = rcopy(st_hbm, rv_st.at[core], 2, pair)
+    near_ad = rcopy(ad_hbm, rv_ad.at[core], 3, pair)
+    for cp in loads:
+        cp.wait()
 
     for cp in halo_copies:
         cp.wait_recv()
@@ -265,13 +274,13 @@
     res, adj = pl.pallas_call(
         kern,
         out_shape=(block, block),
-        in_specs=[pl.BlockSpec(memory_space=pltpu.SMEM)] * 2 + [vmem, vmem],
+        in_specs=[pl.BlockSpec(memory_space=pltpu.SMEM)] * 2 + [pl.BlockSpec(memory_space=pl.ANY)] * 2,
         out_specs=(pl.BlockSpec(memory_space=pl.ANY),) * 2,
-        scratch_shapes=[pltpu.VMEM(state.shape, jnp.float32)] * 2
+        scratch_shapes=[pltpu.VMEM(state.shape, jnp.float32)] * 4
         + [pltpu.VMEM((2,) + state.shape, jnp.float32)] * 2
         + [pltpu.VMEM(halo_shape, jnp.float32)] * 2
         + [pltpu.SemaphoreType.DMA((6 + 2 * comp,)), pltpu.SemaphoreType.DMA((6 + 2 * comp,))]
-        + [pltpu.SemaphoreType.DMA((2 * comp,))],
+        + [pltpu.SemaphoreType.DMA((2 * comp,)), pltpu.SemaphoreType.DMA((2,))],
         compiler_params=pltpu.CompilerParams(collective_id=0, has_side_effects=True),
     )(plan, valve, state, adjoint)
     return res, adj

time: 48.6 us -> 48.2 us (level)
  no operation moved by 1% of the time
where the time goes in v11:
time: 48.2 us; the launch traced here: 48.1 us
  Pallas kernels  44.4 us (92%)
  local copies, waits for them, and re-layouts  3.04 us (6%)
  between operations  0.65 us (1%)
    pallas_call x1, Pallas kernels, local(): pl.pallas_call(kern, out_shape=(block, block), in_specs=[pl.BlockSpec(mem...  44.4 us
    unnamed x4, local copies, waits for them, and re-layouts  3.04 us

profile of v11, /device:TPU:1, one launch (start us, length us, event | category | flops | bytes accessed | tf_op | source)
XLA Modules:
  0.0 48.1 jit_solution(13847074666137077070)
XLA Ops:
  0.6 44.4 %shard_map.59 = (f32[4,6,4,16,128]{4,3,2,1,0:T(8,128)}, f32[4,6,4,16,128]{4,3,2,1,0:T(8,128)}) custom-call(s32[4,4]{1,0:T(4,128)} %refs_0_.1, s32[4,4]{1,0:T(4,128)} %refs_1_.1, f32[4,6,4,16,128]{4,3,2,1,0:T(8,128)} %refs_2_.1, f32[4,6,4,16,128]{4,3,2,1,0:T(8,128)} %refs_3_.1), custom_call_target="tpu_custom_call" | custom-call | tf_op jit(solution)/shard_map/pallas_call | solution.py:274
  45.0 0.0 copy-start
  45.0 2.2 %copy.8 = f32[4,6,4,16,128]{4,3,2,1,0:T(8,128)} copy(f32[4,6,4,16,128]{4,3,2,1,0:T(8,128)} %get-tuple-element.4) | data formatting | bytes 1572864
  47.2 0.0 copy-done
  47.2 0.9 %copy.9 = f32[4,6,4,16,128]{4,3,2,1,0:T(8,128)} copy(f32[4,6,4,16,128]{4,3,2,1,0:T(8,128)S(1)} %copy-done) | data formatting | bytes 1572864
Async XLA Ops:
  45.0 2.2 %copy-start = (f32[4,6,4,16,128]{4,3,2,1,0:T(8,128)S(1)}, f32[4,6,4,16,128]{4,3,2,1,0:T(8,128)}, u32[]{:S(2)}) copy-start(f32[4,6,4,16,128]{4,3,2,1,0:T(8,128)} %get-tuple-element.5) | copy-start | bytes 2359300

commit v12 on v11

--- a/solution.py
+++ b/solution.py
@@ -20,7 +20,7 @@
 MESH = pl.DeviceIdType.MESH
 
 
-def _kernel(n_tm, plan, valve, st_hbm, ad_hbm, res_out, adj_out, st, ad, res, adj, rv_st, rv_ad, h_st, h_ad, send, recv, osem, lsem):
+def _kernel(n_tm, plan, valve, st_hbm, ad_hbm, res, adj, st, ad, rv_st, rv_ad, h_st, h_ad, send, recv, lsem):
     inst, comp, beds, nz, nr = st.shape
     me = lax.axis_index("tm")
     sec = lax.axis_index("sec")
@@ -225,12 +225,6 @@
     def _():
         time_pass(True, False)
 
-    def out_descs(c):
-        return (
-            pltpu.make_async_copy(res.at[:, c], res_out.at[:, c], osem.at[c]),
-            pltpu.make_async_copy(adj.at[:, c], adj_out.at[:, c], osem.at[comp + c]),
-        )
-
     def far_body(c, carry):
         for cp in far_descs(c):
             cp.wait_recv()
@@ -243,15 +237,11 @@
         def _():
             time_pass(True, True, c)
 
-        for cp in out_descs(c):
-            cp.start()
         return carry
 
     lax.fori_loop(0, comp, far_body, 0)
 
     def drain(c, carry):
-        for cp in out_descs(c):
-            cp.wait()
         for cp in far_descs(c):
             cp.wait_send()
         return carry
@@ -273,14 +263,14 @@
 
     res, adj = pl.pallas_call(
         kern,
-        out_shape=(block, block),
+        out_shape=(pltpu.VMEM(state.shape, jnp.float32),) * 2,
         in_specs=[pl.BlockSpec(memory_space=pltpu.SMEM)] * 2 + [pl.BlockSpec(memory_space=pl.ANY)] * 2,
-        out_specs=(pl.BlockSpec(memory_space=pl.ANY),) * 2,
-        scratch_shapes=[pltpu.VMEM(state.shape, jnp.float32)] * 4
+        out_specs=(vmem, vmem),
+        scratch_shapes=[pltpu.VMEM(state.shape, jnp.float32)] * 2
         + [pltpu.VMEM((2,) + state.shape, jnp.float32)] * 2
         + [pltpu.VMEM(halo_shape, jnp.float32)] * 2
         + [pltpu.SemaphoreType.DMA((6 + 2 * comp,)), pltpu.SemaphoreType.DMA((6 + 2 * comp,))]
-        + [pltpu.SemaphoreType.DMA((2 * comp,)), pltpu.SemaphoreType.DMA((2,))],
+        + [pltpu.SemaphoreType.DMA((2,))],
         compiler_params=pltpu.CompilerParams(collective_id=0, has_side_effects=True),
     )(plan, valve, state, adjoint)
     return res, adj

time: 48.2 us -> 46.1 us (0.956)
  local copies, waits for them, and re-layouts: 3.04 us -> 1.76 us
  Pallas kernels: 44.4 us -> 43.6 us
    unnamed x4 -> x2, local copies, waits for them, and re-layouts: 3.04 us -> 1.76 us
    pallas_call x1, Pallas kernels: 44.4 us -> 43.6 us  [local(): pl.pallas_call(kern, out_shape=(pltpu.VMEM(state.shape, jnp.float32),) *...]
where the time goes in v12:
time: 46.1 us; the launch traced here: 46 us
  Pallas kernels  43.6 us (95%)
  local copies, waits for them, and re-layouts  1.76 us (4%)
  between operations  0.64 us (1%)
    pallas_call x1, Pallas kernels, local(): pl.pallas_call(kern, out_shape=(pltpu.VMEM(state.shape, jnp.float32),) *...  43.6 us
    unnamed x2, local copies, waits for them, and re-layouts  1.76 us

profile of v12, /device:TPU:1, one launch (start us, length us, event | category | flops | bytes accessed | tf_op | source)
XLA Modules:
  0.0 46.0 jit_solution(14965561235526563922)
XLA Ops:
  0.6 43.6 %shard_map.59 = (f32[4,6,4,16,128]{4,3,2,1,0:T(8,128)S(1)}, f32[4,6,4,16,128]{4,3,2,1,0:T(8,128)S(1)}) custom-call(s32[4,4]{1,0:T(4,128)} %refs_0_.1, s32[4,4]{1,0:T(4,128)} %refs_1_.1, f32[4,6,4,16,128]{4,3,2,1,0:T(8,128)} %refs_2_.1, f32[4,6,4,16,128]{4,3,2,1,0:T(8,128)} %refs_3_.1), custom_call_target="tpu_custom_call" | custom-call | tf_op jit(solution)/shard_map/pallas_call | solution.py:264
  44.2 0.9 %copy.8 = f32[4,6,4,16,128]{4,3,2,1,0:T(8,128)} copy(f32[4,6,4,16,128]{4,3,2,1,0:T(8,128)S(1)} %get-tuple-element.2) | data formatting | bytes 1572864
  45.1 0.9 %copy.9 = f32[4,6,4,16,128]{4,3,2,1,0:T(8,128)} copy(f32[4,6,4,16,128]{4,3,2,1,0:T(8,128)S(1)} %get-tuple-element.3) | data formatting | bytes 1572864

commit v13 on v12

--- a/solution.py
+++ b/solution.py
@@ -20,8 +20,10 @@
 MESH = pl.DeviceIdType.MESH
 
 
-def _kernel(n_tm, plan, valve, st_hbm, ad_hbm, res, adj, st, ad, rv_st, rv_ad, h_st, h_ad, send, recv, lsem):
+def _kernel(n_tm, plan, valve, st_hbm, ad_hbm, both, st, ad, rv_st, rv_ad, h_st, h_ad, send, recv, lsem):
     inst, comp, beds, nz, nr = st.shape
+    res = both.at[0]
+    adj = both.at[1]
     me = lax.axis_index("tm")
     sec = lax.axis_index("sec")
     core = lax.rem(me, 2)
@@ -261,11 +263,11 @@
     def kern(*refs):
         _kernel(n_tm, *refs)
 
-    res, adj = pl.pallas_call(
+    both = pl.pallas_call(
         kern,
-        out_shape=(pltpu.VMEM(state.shape, jnp.float32),) * 2,
+        out_shape=pltpu.VMEM((2,) + state.shape, jnp.float32),
         in_specs=[pl.BlockSpec(memory_space=pltpu.SMEM)] * 2 + [pl.BlockSpec(memory_space=pl.ANY)] * 2,
-        out_specs=(vmem, vmem),
+        out_specs=vmem,
         scratch_shapes=[pltpu.VMEM(state.shape, jnp.float32)] * 2
         + [pltpu.VMEM((2,) + state.shape, jnp.float32)] * 2
         + [pltpu.VMEM(halo_shape, jnp.float32)] * 2
@@ -273,7 +275,7 @@
         + [pltpu.SemaphoreType.DMA((2,))],
         compiler_params=pltpu.CompilerParams(collective_id=0, has_side_effects=True),
     )(plan, valve, state, adjoint)
-    return res, adj
+    return both[0], both[1]
 
 
 def solution(mesh):

time: 46.1 us -> 45.6 us (0.989)
  local copies, waits for them, and re-layouts: 1.76 us -> 1.25 us
    unnamed x2 -> x0, local copies, waits for them, and re-layouts: 1.76 us -> none
    squeeze x0 -> x1, local copies, waits for them, and re-layouts: none -> 1.25 us  [local(): return (both[0], both[1])]
where the time goes in v13:
time: 45.6 us; the launch traced here: 45.5 us
  Pallas kernels  43.6 us (96%)
  local copies, waits for them, and re-layouts  1.25 us (3%)
  between operations  0.64 us (1%)
    pallas_call x1, Pallas kernels, local(): pl.pallas_call(kern, out_shape=pltpu.VMEM((2,) + state.shape, jnp.float32...  43.6 us
    squeeze x1, local copies, waits for them, and re-layouts, local(): return (both[0], both[1])  1.25 us

profile of v13, /device:TPU:1, one launch (start us, length us, event | category | flops | bytes accessed | tf_op | source)
XLA Modules:
  0.0 45.5 jit_solution(9454961062133598641)
XLA Ops:
  0.6 43.6 %shard_map.59 = f32[2,4,6,4,16,128]{5,4,3,2,1,0:T(8,128)S(1)} custom-call(s32[4,4]{1,0:T(4,128)} %refs_0_.1, s32[4,4]{1,0:T(4,128)} %refs_1_.1, f32[4,6,4,16,128]{4,3,2,1,0:T(8,128)} %refs_2_.1, f32[4,6,4,16,128]{4,3,2,1,0:T(8,128)} %refs_3_.1), custom_call_target="tpu_custom_call" | custom-call | tf_op jit(solution)/shard_map/pallas_call | solution.py:266
  44.2 1.2 %slice_bitcast_fusion = (f32[4,6,4,16,128]{4,3,2,1,0:T(8,128)}, f32[4,6,4,16,128]{4,3,2,1,0:T(8,128)}) fusion(f32[2,4,6,4,16,128]{5,4,3,2,1,0:T(8,128)S(1)} %shard_map.59), kind=kLoop, calls=%fused_computation | loop fusion | bytes 3145728 | tf_op jit(solution)/shard_map/squeeze | solution.py:278

commit v14 on v13

--- a/solution.py
+++ b/solution.py
@@ -68,9 +68,9 @@
             desc(ad_hbm.at[:, c], rv_ad.at[1 - core, :, c], 6 + comp + c, cross),
         )
 
-    for c in range(comp):
-        for cp in far_descs(c):
-            cp.start()
+    for i in range(2):
+        for c in range(comp):
+            far_descs(c)[i].start()
     near_st = rcopy(st_hbm, rv_st.at[core], 2, pair)
     near_ad = rcopy(ad_hbm, rv_ad.at[core], 3, pair)
     for cp in loads:
@@ -176,39 +176,44 @@
 
         lax.fori_loop(0, inst, purge_body, 0)
 
-    def time_pass(cross_right, use_far, comp_index=None):
+    def time_pass(cross_right, use_far, comp_index=None, arrays=(0, 1)):
+        srcs = ((st, rv_st, res, 1.0), (ad, rv_ad, adj, -1.0))
+
         def body(c, carry):
-            for t in range(inst):
-                acc_s = None
-                acc_a = None
-                for k, w in enumerate(STENCIL):
-                    s = k + 1
-                    d_s = None
-                    d_a = None
-                    for j, sign in ((t + s, 1.0), (t - s, -1.0)):
-                        if j >= inst:
-                            far = cross_right
-                            xs, xa = rv_st[1, j - inst, c], rv_ad[1, j - inst, c]
-                        elif j < 0:
-                            far = not cross_right
-                            xs, xa = rv_st[0, j + inst, c], rv_ad[0, j + inst, c]
-                        else:
-                            far = False
-                            xs, xa = st[j, c], ad[j, c]
-                        if far != use_far:
+            for which in arrays:
+                own, recvd, out, scale = srcs[which]
+                for t in range(inst):
+                    acc = None
+                    for k, w in enumerate(STENCIL):
+                        s = k + 1
+                        d = None
+                        for j, sign in ((t + s, 1.0), (t - s, -1.0)):
+                            if j >= inst:
+                                far = cross_right
+                            elif j < 0:
+                                far = not cross_right
+                            else:
+                                far = False
+                            if far != use_far:
+                                continue
+                            if j >= inst:
+                                x = recvd[1, j - inst, c]
+                            elif j < 0:
+                                x = recvd[0, j + inst, c]
+                            else:
+                                x = own[j, c]
+                            if sign < 0:
+                                x = -x
+                            d = x if d is None else d + x
+                        if d is None:
                             continue
-                        if sign < 0:
-                            xs, xa = -xs, -xa
-                        d_s = xs if d_s is None else d_s + xs
-                        d_a = xa if d_a is None else d_a + xa
-                    if d_s is None:
+                        acc = w * d if acc is None else acc + w * d
+                    if acc is None:
                         continue
-                    acc_s = w * d_s if acc_s is None else acc_s + w * d_s
-                    acc_a = w * d_a if acc_a is None else acc_a + w * d_a
-                if acc_s is None:
-                    continue
-                res[t, c] = TIME_SCALE * acc_s + res[t, c]
-                adj[t, c] = adj[t, c] - TIME_SCALE * acc_a
+                    if scale > 0:
+                        out[t, c] = TIME_SCALE * acc + out[t, c]
+                    else:
+                        out[t, c] = out[t, c] - TIME_SCALE * acc
             return carry
 
         if comp_index is None:
@@ -227,21 +232,21 @@
     def _():
         time_pass(True, False)
 
-    def far_body(c, carry):
-        for cp in far_descs(c):
-            cp.wait_recv()
-
-        @pl.when(core == 0)
-        def _():
-            time_pass(False, True, c)
-
-        @pl.when(core == 1)
-        def _():
-            time_pass(True, True, c)
-
-        return carry
-
-    lax.fori_loop(0, comp, far_body, 0)
+    for i in range(2):
+        def far_body(c, carry, i=i):
+            far_descs(c)[i].wait_recv()
+
+            @pl.when(core == 0)
+            def _():
+                time_pass(False, True, c, (i,))
+
+            @pl.when(core == 1)
+            def _():
+                time_pass(True, True, c, (i,))
+
+            return carry
+
+        lax.fori_loop(0, comp, far_body, 0)
 
     def drain(c, carry):
         for cp in far_descs(c):

time: 45.6 us -> 45.6 us (level)
  no operation moved by 1% of the time
where the time goes in v14:
time: 45.6 us; the launch traced here: 45.5 us
  Pallas kernels  43.6 us (96%)
  local copies, waits for them, and re-layouts  1.25 us (3%)
  between operations  0.64 us (1%)
    pallas_call x1, Pallas kernels, local(): pl.pallas_call(kern, out_shape=pltpu.VMEM((2,) + state.shape, jnp.float32...  43.6 us
    squeeze x1, local copies, waits for them, and re-layouts, local(): return (both[0], both[1])  1.25 us

profile of v14, /device:TPU:1, one launch (start us, length us, event | category | flops | bytes accessed | tf_op | source)
XLA Modules:
  0.0 45.5 jit_solution(15526520268293840019)
XLA Ops:
  0.6 43.6 %shard_map.59 = f32[2,4,6,4,16,128]{5,4,3,2,1,0:T(8,128)S(1)} custom-call(s32[4,4]{1,0:T(4,128)} %refs_0_.1, s32[4,4]{1,0:T(4,128)} %refs_1_.1, f32[4,6,4,16,128]{4,3,2,1,0:T(8,128)} %refs_2_.1, f32[4,6,4,16,128]{4,3,2,1,0:T(8,128)} %refs_3_.1), custom_call_target="tpu_custom_call" | custom-call | tf_op jit(solution)/shard_map/pallas_call | solution.py:271
  44.2 1.2 %slice_bitcast_fusion = (f32[4,6,4,16,128]{4,3,2,1,0:T(8,128)}, f32[4,6,4,16,128]{4,3,2,1,0:T(8,128)}) fusion(f32[2,4,6,4,16,128]{5,4,3,2,1,0:T(8,128)S(1)} %shard_map.59), kind=kLoop, calls=%fused_computation | loop fusion | bytes 3145728 | tf_op jit(solution)/shard_map/squeeze | solution.py:283

commit v15 on v14

--- a/solution.py
+++ b/solution.py
@@ -258,6 +258,17 @@
         cp.wait_send()
 
 
+def _store(both, res_out, adj_out, sem):
+    copies = [
+        pltpu.make_async_copy(both.at[0], res_out, sem.at[0]),
+        pltpu.make_async_copy(both.at[1], adj_out, sem.at[1]),
+    ]
+    for cp in copies:
+        cp.start()
+    for cp in copies:
+        cp.wait()
+
+
 def local(state, adjoint, plan, valve):
     n_tm = lax.axis_size("tm")
     inst, comp, beds, nz, nr = state.shape
@@ -280,7 +291,14 @@
         + [pltpu.SemaphoreType.DMA((2,))],
         compiler_params=pltpu.CompilerParams(collective_id=0, has_side_effects=True),
     )(plan, valve, state, adjoint)
-    return both[0], both[1]
+    hbm = pl.BlockSpec(memory_space=pl.ANY)
+    return pl.pallas_call(
+        _store,
+        out_shape=(block, block),
+        in_specs=[vmem],
+        out_specs=(hbm, hbm),
+        scratch_shapes=[pltpu.SemaphoreType.DMA((2,))],
+    )(pltpu.with_memory_space_constraint(both, pltpu.VMEM))
 
 
 def solution(mesh):

time: 45.6 us -> 45.5 us (level)
  local copies, waits for them, and re-layouts: 1.25 us -> 0 us
  Pallas kernels: 43.6 us -> 44.7 us
    squeeze x1 -> x0, local copies, waits for them, and re-layouts: 1.25 us -> none  [local(): return (both[0], both[1])]
    pallas_call x0 -> x1, Pallas kernels: none -> 1.16 us  [local(): pl.pallas_call(_store, out_shape=(block, block), in_specs=[vmem], out_spe...]
where the time goes in v15:
time: 45.5 us; the launch traced here: 45.4 us
  Pallas kernels  44.7 us (98%)
  between operations  0.64 us (1%)
    pallas_call x1, Pallas kernels, local(): pl.pallas_call(kern, out_shape=pltpu.VMEM((2,) + state.shape, jnp.float32...  43.6 us
    pallas_call x1, Pallas kernels, local(): pl.pallas_call(_store, out_shape=(block, block), in_specs=[vmem], out_spe...  1.16 us

profile of v15, /device:TPU:1, one launch (start us, length us, event | category | flops | bytes accessed | tf_op | source)
XLA Modules:
  0.0 45.4 jit_solution(9690926607279406901)
XLA Ops:
  0.6 43.6 %shard_map.59.both = f32[2,4,6,4,16,128]{5,4,3,2,1,0:T(8,128)S(1)} custom-call(s32[4,4]{1,0:T(4,128)} %refs_0_.1, s32[4,4]{1,0:T(4,128)} %refs_1_.1, f32[4,6,4,16,128]{4,3,2,1,0:T(8,128)} %refs_2_.1, f32[4,6,4,16,128]{4,3,2,1,0:T(8,128)} %refs_3_.1), custom_call_target="tpu_custom_call" | custom-call | tf_op jit(solution)/shard_map/pallas_call | solution.py:282
  44.2 1.2 %shard_map.60 = (f32[4,6,4,16,128]{4,3,2,1,0:T(8,128)}, f32[4,6,4,16,128]{4,3,2,1,0:T(8,128)}) custom-call(f32[2,4,6,4,16,128]{5,4,3,2,1,0:T(8,128)S(1)} %shard_map.59.both), custom_call_target="tpu_custom_call" | custom-call | tf_op jit(solution)/shard_map/pallas_call | solution.py:295

commit v16 on v15

--- a/solution.py
+++ b/solution.py
@@ -259,9 +259,11 @@
 
 
 def _store(both, res_out, adj_out, sem):
+    inst = res_out.shape[0]
     copies = [
-        pltpu.make_async_copy(both.at[0], res_out, sem.at[0]),
-        pltpu.make_async_copy(both.at[1], adj_out, sem.at[1]),
+        pltpu.make_async_copy(both.at[i, t], out.at[t], sem.at[i * inst + t])
+        for i, out in enumerate((res_out, adj_out))
+        for t in range(inst)
     ]
     for cp in copies:
         cp.start()
@@ -297,7 +299,7 @@
         out_shape=(block, block),
         in_specs=[vmem],
         out_specs=(hbm, hbm),
-        scratch_shapes=[pltpu.SemaphoreType.DMA((2,))],
+        scratch_shapes=[pltpu.SemaphoreType.DMA((2 * inst,))],
     )(pltpu.with_memory_space_constraint(both, pltpu.VMEM))
 
 

time: 45.5 us -> 45.5 us (level)
  no operation moved by 1% of the time
where the time goes in v16:
time: 45.5 us; the launch traced here: 45.4 us
  Pallas kernels  44.8 us (98%)
  between operations  0.64 us (1%)
    pallas_call x1, Pallas kernels, local(): pl.pallas_call(kern, out_shape=pltpu.VMEM((2,) + state.shape, jnp.float32...  43.6 us
    pallas_call x1, Pallas kernels, local(): pl.pallas_call(_store, out_shape=(block, block), in_specs=[vmem], out_spe...  1.2 us

profile of v16, /device:TPU:1, one launch (start us, length us, event | category | flops | bytes accessed | tf_op | source)
XLA Modules:
  0.0 45.4 jit_solution(8122307177009526102)
XLA Ops:
  0.6 43.6 %shard_map.59.both = f32[2,4,6,4,16,128]{5,4,3,2,1,0:T(8,128)S(1)} custom-call(s32[4,4]{1,0:T(4,128)} %refs_0_.1, s32[4,4]{1,0:T(4,128)} %refs_1_.1, f32[4,6,4,16,128]{4,3,2,1,0:T(8,128)} %refs_2_.1, f32[4,6,4,16,128]{4,3,2,1,0:T(8,128)} %refs_3_.1), custom_call_target="tpu_custom_call" | custom-call | tf_op jit(solution)/shard_map/pallas_call | solution.py:284
  44.2 1.2 %shard_map.60 = (f32[4,6,4,16,128]{4,3,2,1,0:T(8,128)}, f32[4,6,4,16,128]{4,3,2,1,0:T(8,128)}) custom-call(f32[2,4,6,4,16,128]{5,4,3,2,1,0:T(8,128)S(1)} %shard_map.59.both), custom_call_target="tpu_custom_call" | custom-call | tf_op jit(solution)/shard_map/pallas_call | solution.py:297

commit v17 on v14

--- a/solution.py
+++ b/solution.py
@@ -31,13 +31,6 @@
     cross = (lax.rem(me + 2 * core - 1 + n_tm, n_tm), sec)
     partner = (me, 1 - sec)
 
-    loads = [
-        pltpu.make_async_copy(st_hbm, st, lsem.at[0]),
-        pltpu.make_async_copy(ad_hbm, ad, lsem.at[1]),
-    ]
-    for cp in loads:
-        cp.start()
-
     barrier = pltpu.get_barrier_semaphore()
     for dev in (pair, cross, partner):
         pl.semaphore_signal(barrier, inc=1, device_id=dev, device_id_type=MESH)
@@ -51,26 +44,32 @@
         cp.start()
         return cp
 
+    def desc(src, dst, i, dev):
+        return pltpu.make_async_remote_copy(
+            src_ref=src, dst_ref=dst, send_sem=send.at[i], recv_sem=recv.at[i],
+            device_id=dev, device_id_type=MESH,
+        )
+
+    def far_descs(c):
+        return (
+            desc(st_hbm.at[:, c], rv_st.at[1 - core, :, c], 6 + c, cross),
+            desc(ad_hbm.at[:, c], rv_ad.at[1 - core, :, c], 6 + comp + c, cross),
+        )
+
+    for i in range(2):
+        for c in range(comp):
+            far_descs(c)[i].start()
     row_src = (nz - 1) * (1 - sec)
     halo_copies = [
         rcopy(src.at[:, :, :, pl.ds(row_src, 1), :], dst.at[:, :, :, pl.ds(0, 1), :], 4 + i, partner)
         for i, (src, dst) in enumerate(((st_hbm, h_st), (ad_hbm, h_ad)))
     ]
-    def desc(src, dst, i, dev):
-        return pltpu.make_async_remote_copy(
-            src_ref=src, dst_ref=dst, send_sem=send.at[i], recv_sem=recv.at[i],
-            device_id=dev, device_id_type=MESH,
-        )
-
-    def far_descs(c):
-        return (
-            desc(st_hbm.at[:, c], rv_st.at[1 - core, :, c], 6 + c, cross),
-            desc(ad_hbm.at[:, c], rv_ad.at[1 - core, :, c], 6 + comp + c, cross),
-        )
-
-    for i in range(2):
-        for c in range(comp):
-            far_descs(c)[i].start()
+    loads = [
+        pltpu.make_async_copy(st_hbm, st, lsem.at[0]),
+        pltpu.make_async_copy(ad_hbm, ad, lsem.at[1]),
+    ]
+    for cp in loads:
+        cp.start()
     near_st = rcopy(st_hbm, rv_st.at[core], 2, pair)
     near_ad = rcopy(ad_hbm, rv_ad.at[core], 3, pair)
     for cp in loads:

time: 45.6 us -> 47.2 us (1.035)
  Pallas kernels: 43.6 us -> 45.2 us
    pallas_call x1, Pallas kernels: 43.6 us -> 45.2 us  [local(): pl.pallas_call(kern, out_shape=pltpu.VMEM((2,) + state.shape, jnp.float32...]
where the time goes in v17:
time: 47.2 us; the launch traced here: 47.1 us
  Pallas kernels  45.2 us (96%)
  local copies, waits for them, and re-layouts  1.25 us (3%)
  between operations  0.64 us (1%)
    pallas_call x1, Pallas kernels, local(): pl.pallas_call(kern, out_shape=pltpu.VMEM((2,) + state.shape, jnp.float32...  45.2 us
    squeeze x1, local copies, waits for them, and re-layouts, local(): return (both[0], both[1])  1.25 us

profile of v17, /device:TPU:1, one launch (start us, length us, event | category | flops | bytes accessed | tf_op | source)
XLA Modules:
  0.0 47.1 jit_solution(15721196159356472807)
XLA Ops:
  0.6 45.2 %shard_map.59 = f32[2,4,6,4,16,128]{5,4,3,2,1,0:T(8,128)S(1)} custom-call(s32[4,4]{1,0:T(4,128)} %refs_0_.1, s32[4,4]{1,0:T(4,128)} %refs_1_.1, f32[4,6,4,16,128]{4,3,2,1,0:T(8,128)} %refs_2_.1, f32[4,6,4,16,128]{4,3,2,1,0:T(8,128)} %refs_3_.1), custom_call_target="tpu_custom_call" | custom-call | tf_op jit(solution)/shard_map/pallas_call | solution.py:270
  45.8 1.2 %slice_bitcast_fusion = (f32[4,6,4,16,128]{4,3,2,1,0:T(8,128)}, f32[4,6,4,16,128]{4,3,2,1,0:T(8,128)}) fusion(f32[2,4,6,4,16,128]{5,4,3,2,1,0:T(8,128)S(1)} %shard_map.59), kind=kLoop, calls=%fused_computation | loop fusion | bytes 3145728 | tf_op jit(solution)/shard_map/squeeze | solution.py:282
